TPU v7x, 32 devices: a whole 2x2x4 slice. The times are simulated.
32 devices in a mesh: groups: 2 (over x), ctx: 16 (over z, y, core).
Axes of the slice: x: 2, y: 2, z: 4, core: 2. Of those that a mesh axis runs over, the one named last changes fastest.
Arguments:
- queries: bfloat16 [64, 8192], P(('groups', 'ctx')), parts along dimension 0, may hold values from -256 to 256, as said below
- cached_key_rows: bfloat16 [16384, 1024], P(('groups', 'ctx')), parts along dimension 0, may hold values from -4 to 4, as said below
- cached_value_rows: bfloat16 [16384, 1024], P(('groups', 'ctx')), parts along dimension 0, may hold values from -6 to 6
- cache_position: int32 [16384], P(('groups', 'ctx')), parts along dimension 0, may hold values from 0 to 8191, as said below
- lengths: int32 [64], P(('groups', 'ctx')), parts along dimension 0, may hold values from 2 to 8192, as said below
- norm_gain: float32 [8192], replicated, may hold values from 0.5 to 1.5
- gate_weight: bfloat16 [14336, 8192], P('ctx'), may hold values from -0.0625 to 0.0625
- up_weight: bfloat16 [14336, 8192], P('ctx'), may hold values from -0.0625 to 0.0625
- down_weight: bfloat16 [14336, 8192], P('ctx'), may hold values from -0.046875 to 0.046875
Outputs:
- layer_out: bfloat16 [64, 8192], P(('groups', 'ctx')), parts along dimension 0
There are 2 independent parts, one for each index of `groups`. A program takes and returns all parts, laid end to end along the dimension named above; an argument that names none is the same for every part. Nothing has to cross between parts.
Inputs may be any that keep to these rules, and one draw needn't show every extreme that they name: `queries`: queries stay within the stated range. `cached_key_rows`: keys stay within the stated range. `cache_position`: A permutation of 0 to 8191. `lengths`: some row has length 8192 and some row has length 2.
All inputs are finite; a program needn't handle non-finite values.
Results may differ from a plain program's by a relative error of at most 0.02.
Values may be sent and summed in bfloat16 or wider, within the bound.
No kernel may reach another device: no remote copies, remote signals or barrier semaphores. Data moves between devices by JAX's collectives and lax.ppermute only.
A program may use at most 128 MiB of HBM per device.

v0:
```python
import jax
import jax.numpy as jnp
from jax import lax
from jax.sharding import PartitionSpec as P

D = 8192
QUERY_HEADS = 64
KEY_VALUE_HEADS = 8
HEAD_SIZE = 128


def partial_softmax(
    query_row_matrix, row_lengths, cached_key_rows, cached_value_rows, cache_position
):
    count_of_rows = query_row_matrix.shape[0]
    count_of_slots = cached_key_rows.shape[0]
    query_group_size = QUERY_HEADS // KEY_VALUE_HEADS
    query_head_count = query_row_matrix.reshape(
        count_of_rows, KEY_VALUE_HEADS, query_group_size, HEAD_SIZE
    )
    key_head_count = cached_key_rows.reshape(count_of_slots, KEY_VALUE_HEADS, HEAD_SIZE)
    value_head_count = cached_value_rows.reshape(count_of_slots, KEY_VALUE_HEADS, HEAD_SIZE)
    scores = jnp.einsum(
        "rkgd,tkd->rkgt", query_head_count, key_head_count, preferred_element_type=jnp.float32
    ) * HEAD_SIZE ** (-0.5)
    live = (cache_position[None, :] < row_lengths[:, None])[:, None, None, :]
    scores = jnp.where(live, scores, -1e30)
    peak = jnp.max(scores, axis=3)
    weights = jnp.where(live, jnp.exp(scores - peak[..., None]), 0.0)
    totals = jnp.sum(weights, axis=3)
    summed = jnp.einsum(
        "rkgt,tkd->rkgd",
        weights.astype(jnp.bfloat16),
        value_head_count,
        preferred_element_type=jnp.float32,
    )
    return (
        peak.reshape(count_of_rows, QUERY_HEADS),
        totals.reshape(count_of_rows, QUERY_HEADS),
        summed.reshape(count_of_rows, QUERY_HEADS, HEAD_SIZE),
    )


def local(
    queries,
    cached_key_rows,
    cached_value_rows,
    cache_position,
    lengths,
    norm_gain,
    gate_weight,
    up_weight,
    down_weight,
):
    cycle_size = lax.axis_size("ctx")
    row_dev = queries.shape[0]
    all_lengths = lax.all_gather(lengths, "ctx", axis=0, tiled=True)
    every_query = lax.all_gather(queries, "ctx", axis=0, tiled=True)
    count_of_blocks = cycle_size // 8
    block_rows = row_dev * 8

    def one_block(pieces):
        return partial_softmax(
            pieces[0], pieces[1], cached_key_rows, cached_value_rows, cache_position
        )

    peak_all, totals_all, summed_all = lax.map(
        one_block,
        (
            every_query.reshape(count_of_blocks, block_rows, D),
            all_lengths.reshape(count_of_blocks, block_rows),
        ),
    )
    peak_all = peak_all.reshape(cycle_size, row_dev, QUERY_HEADS)
    totals_all = totals_all.reshape(cycle_size, row_dev, QUERY_HEADS)
    summed_all = summed_all.reshape(cycle_size, row_dev, QUERY_HEADS, HEAD_SIZE)
    peak_all, totals_all, summed_all = (
        lax.all_to_all(peak_all, "ctx", split_axis=0, concat_axis=0, tiled=True),
        lax.all_to_all(totals_all, "ctx", split_axis=0, concat_axis=0, tiled=True),
        lax.all_to_all(summed_all, "ctx", split_axis=0, concat_axis=0, tiled=True),
    )
    peak = jnp.max(peak_all, axis=0)
    scaling = jnp.exp(peak_all - peak[None])
    totals = jnp.sum(totals_all * scaling, axis=0)
    summed = jnp.sum(summed_all * scaling[..., None], axis=0)
    attended = (summed / totals[..., None]).reshape(row_dev, D).astype(jnp.bfloat16)
    widened = attended.astype(jnp.float32)
    mean_square = jnp.mean(widened * widened, axis=1, keepdims=True) + 1e-05
    normed = (widened * lax.rsqrt(mean_square) * norm_gain[None, :]).astype(jnp.bfloat16)
    piece = lax.all_gather(normed, "ctx", axis=0, tiled=True)
    gate = lax.dot_general(
        piece, gate_weight, (((1,), (1,)), ((), ())), preferred_element_type=jnp.float32
    )
    upward = lax.dot_general(
        piece, up_weight, (((1,), (1,)), ((), ())), preferred_element_type=jnp.float32
    )
    activated = (jax.nn.silu(gate) * upward).astype(jnp.bfloat16)
    layer_sum = lax.psum_scatter(
        jnp.dot(activated, down_weight, preferred_element_type=jnp.float32),
        "ctx",
        scatter_dimension=0,
        tiled=True,
    )
    return layer_sum.astype(jnp.bfloat16)


def solution(mesh):
    placed = (
        P(("groups", "ctx"), None),
        P(("groups", "ctx"), None),
        P(("groups", "ctx"), None),
        P(("groups", "ctx")),
        P(("groups", "ctx")),
        P(),
        P("ctx", None),
        P("ctx", None),
        P("ctx", None),
    )
    return jax.shard_map(
        local, mesh=mesh, in_specs=placed, out_specs=P(("groups", "ctx"), None), check_vma=False
    )
```

profile of v0, /device:TPU:0, one launch (start us, length us, event | category | flops | bytes accessed | tf_op | source)
XLA Modules:
  0.0 214.6 jit_solution(2000556180046539603)
XLA Ops:
  0.0 1.4 fusion.32
  2.0 0.9 dynamic-update-slice
  2.8 13.8 %all-reduce = s32[32]{0:T(128)S(1)} all-reduce(s32[32]{0:T(128)S(1)} %dynamic-update-slice), channel_id=1, replica_groups=mesh['groups'=2,'ctx'=16] {'ctx'}, use_global_device_ids=true, to_apply=%add | all-reduce | flops 32 | bytes 256
  16.7 19.6 %all-gather = bf16[16,2,8192]{2,1,0:T(2,128)(2,1)S(1)} all-gather(bf16[1,2,8192]{2,1,0:T(2,128)(2,1)} %bitcast.91), channel_id=1, replica_groups=mesh['groups'=2,'ctx'=16] {'ctx'}, dimensions={0}, use_global_device_ids=true | all-gather | bytes 557056 | tf_op jit(solution)/shard_map/all_gather | solution.py:58
  36.5 13.3 %while.14 = (s32[]{:T(128)}, f32[2,16,64]{2,1,0:T(8,128)S(1)}, f32[2,16,64]{2,1,0:T(8,128)S(1)}, f32[2,16,64,128]{3,2,1,0:T(8,128)}, s32[512]{0:T(512)}, /*index...) while((s32[]{:T(128)}, f32[2,16,64]{2,1,0:T(8,128)S(1)}, ...), condition=%wide.region_3.4_spmd, body=%wide.region_0.3_spmd.sunk | while | flops 275257344 | bytes 19778380 | solution.py:67
  36.5 0.8 broadcast_compare_fusion.2
  37.3 1.5 copy.79
  38.9 0.6 bitcast_reduce_fusion.2
  39.5 0.6 copy-done
  40.4 0.8 convolution_bitcast_fusion.2
  41.2 0.8 bitcast_dynamic-update-slice_fusion.2
  42.1 0.8 fusion.46
  43.2 0.8 broadcast_compare_fusion.2
  44.0 1.5 copy.79
  45.5 0.6 bitcast_reduce_fusion.2
  46.2 0.6 copy-done
  47.0 0.8 convolution_bitcast_fusion.2
  47.9 0.9 bitcast_dynamic-update-slice_fusion.2
  48.7 0.8 fusion.46
  49.8 0.7 reshape.97
  50.5 3.5 %all-to-all-start.1 = ((f32[16,1,128]{2,1,0:T(1,128)}), f32[16,1,128]{2,1,0:T(1,128)S(1)}, u32[]{:S(2)}, u32[]{:S(2)}) async-start(f32[16,1,128]{2,1,0:T(1,128)} %reshape.97), calls=%async_computation.1 | async-start | bytes 16384 | tf_op jit(solution)/shard_map/all_to_all | solution.py:78
  54.1 6.2 %all-to-all-done.1 = f32[16,1,128]{2,1,0:T(1,128)S(1)} async-done(((f32[16,1,128]{2,1,0:T(1,128)}), f32[16,1,128]{2,1,0:T(1,128)S(1)}, u32[]{:S(2)}, u32[]{:S(2)}) %all-to-all-start.1) | async-done | bytes 8224 | tf_op jit(solution)/shard_map/all_to_all | solution.py:78
  60.3 9.0 %all_to_all.15 = f32[16,1,128]{2,1,0:T(1,128)S(1)} all-to-all(f32[16,1,128]{2,1,0:T(1,128)S(1)} %reshape.99), channel_id=1, replica_groups=mesh['groups'=2,'ctx'=16] {'ctx'}, dimensions={0} | all-to-all | bytes 16384 | tf_op jit(solution)/shard_map/all_to_all | solution.py:79
  69.3 3.7 %all-to-all-start = ((f32[16,2,64,128]{3,2,1,0:T(8,128)}), f32[16,2,64,128]{3,2,1,0:T(8,128)S(1)}, u32[]{:S(2)}, u32[]{:S(2)}) async-start(f32[16,2,64,128]{3,2,1,0:T(8,128)} %bitcast.10), calls=%async_computation | async-start | bytes 2097152 | tf_op jit(solution)/shard_map/all_to_all | solution.py:80
  74.2 0.7 reduce.2
  75.0 0.7 reduce.1
  75.8 20.1 %all-to-all-done = f32[16,2,64,128]{3,2,1,0:T(8,128)S(1)} async-done(((f32[16,2,64,128]{3,2,1,0:T(8,128)}), f32[16,2,64,128]{3,2,1,0:T(8,128)S(1)}, u32[]{:S(2)}, u32[]{:S(2)}) %all-to-all-start) | async-done | bytes 1048608 | tf_op jit(solution)/shard_map/all_to_all | solution.py:80
  96.5 24.0 %all-gather.1 = bf16[16,2,8192]{2,1,0:T(2,128)(2,1)S(1)} all-gather(bf16[1,2,8192]{2,1,0:T(2,128)(2,1)S(1)} %fusion.30), channel_id=1, replica_groups=mesh['groups'=2,'ctx'=16] {'ctx'}, dimensions={0}, use_global_device_ids=true | all-gather | bytes 557056 | tf_op jit(solution)/shard_map/all_gather | solution.py:90
  120.7 9.6 %fusion.33 = f32[32,896]{1,0:T(8,128)S(1)} fusion(bf16[32,8192]{1,0:T(8,128)(2,1)S(1)} %reshape.90, bf16[896,8192]{1,0:T(8,128)(2,1)} %param.17), kind=kOutput, calls=%fused_computation.52 | convolution fusion | flops 469762048 | bytes 15319040 | tf_op jit(solution)/shard_map/dot_general | solution.py:91
  130.3 14.1 %fusion.20 = f32[32,8192]{1,0:T(8,128)S(1)} fusion(bf16[896,8192]{1,0:T(8,128)(2,1)} %param.19, bf16[32,8192]{1,0:T(8,128)(2,1)S(1)} %reshape.90, bf16[896,8192]{1,0:T(8,128)(2,1)} %param.18, f32[32,896]{1,0:T(8,128)S(1)} %fusion.33), kind=kOutput, calls=%fused_computation.31 | convolution fusion | flops 939696128 | bytes 31047680 | tf_op jit(solution)/shard_map/dot_general | solution.py:99
  144.4 69.5 %all-reduce.3 = bf16[32,8192]{1,0:T(8,128)(2,1)S(1)} all-reduce(f32[32,8192]{1,0:T(8,128)S(1)} %fusion.20), channel_id=2, replica_groups=mesh['groups'=2,'ctx'=16] {'ctx'}, use_global_device_ids=true, to_apply=%region_8.9.clone | all-reduce | flops 262144 | bytes 1572864
  213.9 0.7 dynamic-slice_convert_fusion
  (40 shorter events, 3.2 us)
Async XLA Ops:
  38.8 1.2 copy-start
  45.5 1.2 copy-start
  49.8 46.6 %copy-start.1 = (f32[8192]{0:T(1024)S(1)}, f32[8192]{0:T(1024)}, u32[]{:S(2)}) copy-start(f32[8192]{0:T(1024)} %param.16) | copy-start | bytes 98308
  50.5 9.8 %all-to-all-start.1 = ((f32[16,1,128]{2,1,0:T(1,128)}), f32[16,1,128]{2,1,0:T(1,128)S(1)}, u32[]{:S(2)}, u32[]{:S(2)}) async-start(f32[16,1,128]{2,1,0:T(1,128)} %reshape.97), calls=%async_computation.1 | async-start | bytes 16384 | tf_op jit(solution)/shard_map/all_to_all | solution.py:78
  69.3 26.5 %all-to-all-start = ((f32[16,2,64,128]{3,2,1,0:T(8,128)}), f32[16,2,64,128]{3,2,1,0:T(8,128)S(1)}, u32[]{:S(2)}, u32[]{:S(2)}) async-start(f32[16,2,64,128]{3,2,1,0:T(8,128)} %bitcast.10), calls=%async_computation | async-start | bytes 2097152 | tf_op jit(solution)/shard_map/all_to_all | solution.py:80
where the time goes:
time: 215 us
  blocking collectives  136 us (63%)
  matrix products  26.6 us (12%)
  waiting for transfers between devices  26.3 us (12%)
  local copies, waits for them, and re-layouts  12 us (6%)
  starting transfers between devices  7.12 us (3%)
  other arithmetic  5.16 us (2%)
    unnamed x2, blocking collectives  83.3 us
    all_gather x1, blocking collectives, local(): piece = lax.all_gather(normed, 'ctx', axis=0, tiled=True)  24 us
    all_to_all x1, waiting for transfers between devices, local(): lax.all_to_all(summed_all, 'ctx', split_axis=0, concat_axis=0, tiled=True)  20.1 us
    all_gather x1, blocking collectives, local(): every_query = lax.all_gather(queries, 'ctx', axis=0, tiled=True)  19.6 us
    dot_general x1, matrix products, local(): jnp.dot(activated, down_weight, preferred_element_type=jnp.float32)  14.1 us
    dot_general x1, matrix products, local(): lax.dot_general(piece, gate_weight, (((1,), (1,)), ((), ())), preferred_e...  9.59 us
    all_to_all x1, blocking collectives, local(): lax.all_to_all(totals_all, 'ctx', split_axis=0, concat_axis=0, tiled=True)  8.99 us
    all_to_all x1, waiting for transfers between devices, local(): lax.all_to_all(peak_all, 'ctx', split_axis=0, concat_axis=0, tiled=True)  6.23 us
  transfers between devices with their start and end apart: 2, of which 2 were waited for; matrix products, arithmetic and copies ran while one was open for 1% of the time, Pallas kernels for 0%

commit v1 on v0

v1 whole, which is shorter than its diff:
```python
import functools

import jax
import jax.numpy as jnp
from jax import lax
from jax.experimental import pallas as pl
from jax.experimental.pallas import tpu as pltpu
from jax.sharding import PartitionSpec as P

D = 8192
QUERY_HEADS = 64
KEY_VALUE_HEADS = 8
HEAD_SIZE = 128
GROUP = QUERY_HEADS // KEY_VALUE_HEADS
F32 = jnp.float32
BF16 = jnp.bfloat16
ROWS_BY_ROWS = (((1,), (1,)), ((), ()))
VMEM = pl.BlockSpec(memory_space=pltpu.VMEM)
SMEM = pl.BlockSpec(memory_space=pltpu.SMEM)
ANY = pl.BlockSpec(memory_space=pl.ANY)
MIB = 1 << 20


def in_vmem(x):
    return pltpu.with_memory_space_constraint(x, pltpu.VMEM)


def rounded(x):
    return x.astype(BF16).astype(F32)


def pack_kernel(lengths_ref, q_ref, out_ref, slab_ref):
    rows = q_ref.shape[0]
    q = q_ref[...].astype(F32)
    lane = lax.broadcasted_iota(jnp.int32, (GROUP, HEAD_SIZE), 1)
    for row in range(rows):
        for head in range(QUERY_HEADS):
            slot = row * GROUP + head % GROUP
            slab_ref[head // GROUP, slot : slot + 1, :] = q[
                row : row + 1, head * HEAD_SIZE : (head + 1) * HEAD_SIZE
            ]
        length = lengths_ref[row]
        high, low = (length >> 8).astype(F32), (length & 255).astype(F32)
        slab_ref[KEY_VALUE_HEADS, row * GROUP : (row + 1) * GROUP, :] = jnp.where(
            lane == 0, high, jnp.where(lane == 1, low, 0.0)
        )
    packed = slab_ref[...].astype(BF16)
    for peer in range(out_ref.shape[0]):
        out_ref[peer] = packed


def pack(queries, lengths, peers):
    slots = queries.shape[0] * GROUP
    shape = (KEY_VALUE_HEADS + 1, slots, HEAD_SIZE)
    return pl.pallas_call(
        pack_kernel,
        out_shape=pltpu.VMEM((peers,) + shape, BF16),
        in_specs=[SMEM, VMEM],
        out_specs=VMEM,
        scratch_shapes=[pltpu.VMEM(shape, F32)],
        compiler_params=pltpu.CompilerParams(vmem_limit_bytes=4 * MIB),
        name="pack",
    )(lengths, queries)


def attend_kernel(
    near_ref, far_ref, position_ref, k_hbm, v_hbm, w_hbm,
    keep_ref, send_ref, w_ref, k_ref, v_ref, sems,
):
    copies = [
        pltpu.make_async_copy(source, target, sems.at[i])
        for i, (source, target) in enumerate(((k_hbm, k_ref), (v_hbm, v_ref), (w_hbm, w_ref)))
    ]
    for copy in copies:
        copy.start()
    peers, _, slots, _ = near_ref.shape
    half = peers * slots

    def slab(g):
        return jnp.concatenate(
            [ref[:, g].reshape(half, HEAD_SIZE) for ref in (near_ref, far_ref)], axis=0
        )

    numbers = slab(KEY_VALUE_HEADS).astype(F32)
    lengths = numbers[:, 0:1] * 256.0 + numbers[:, 1:2]
    live = position_ref[...].astype(F32) < lengths
    lane = lax.broadcasted_iota(jnp.int32, (2 * half, HEAD_SIZE), 1)
    state = jnp.zeros((2 * half, HEAD_SIZE), F32)
    copies[0].wait()
    copies[1].wait()
    for g in range(KEY_VALUE_HEADS):
        columns = slice(g * HEAD_SIZE, (g + 1) * HEAD_SIZE)
        scores = lax.dot_general(
            slab(g), k_ref[:, columns], ROWS_BY_ROWS, preferred_element_type=F32
        ) * HEAD_SIZE ** (-0.5)
        scores = jnp.where(live, scores, -1e30)
        peak = rounded(jnp.max(scores, axis=1, keepdims=True))
        weights = jnp.where(live, jnp.exp(scores - peak), 0.0)
        total = jnp.sum(weights, axis=1, keepdims=True)
        summed = jnp.dot(weights.astype(BF16), v_ref[:, columns], preferred_element_type=F32)
        total_high = rounded(total)
        for index, column in enumerate((peak, total_high, total - total_high)):
            state = jnp.where(lane == index * KEY_VALUE_HEADS + g, column, state)
        keep_ref[:, g] = summed[:half].reshape(peers, slots, HEAD_SIZE)
        send_ref[:, g] = summed[half:].astype(BF16).reshape(peers, slots, HEAD_SIZE)
    keep_ref[:, KEY_VALUE_HEADS] = state[:half].reshape(peers, slots, HEAD_SIZE)
    send_ref[:, KEY_VALUE_HEADS] = state[half:].astype(BF16).reshape(peers, slots, HEAD_SIZE)
    copies[2].wait()


def attend(near, far, position, keys, values, weight):
    cells = near.size // HEAD_SIZE * keys.shape[0]
    return pl.pallas_call(
        attend_kernel,
        out_shape=(
            pltpu.VMEM(near.shape, F32),
            pltpu.VMEM(near.shape, BF16),
            pltpu.VMEM(weight.shape, weight.dtype),
        ),
        in_specs=[VMEM, VMEM, VMEM, ANY, ANY, ANY],
        out_specs=(VMEM, VMEM, VMEM),
        scratch_shapes=[
            pltpu.VMEM(keys.shape, keys.dtype),
            pltpu.VMEM(values.shape, values.dtype),
            pltpu.SemaphoreType.DMA((3,)),
        ],
        compiler_params=pltpu.CompilerParams(vmem_limit_bytes=20 * MIB),
        cost_estimate=pl.CostEstimate(
            flops=8 * cells * HEAD_SIZE, bytes_accessed=2 * weight.size, transcendentals=2 * cells
        ),
        name="attend",
    )(in_vmem(near), in_vmem(far), position, keys, values, weight)


def state_columns(state, g):
    peak, high, low = (
        state[:, i * KEY_VALUE_HEADS + g : i * KEY_VALUE_HEADS + g + 1] for i in range(3)
    )
    return peak, high + low


def merge_kernel(keep_ref, came_ref, out_ref):
    peers, _, slots, _ = keep_ref.shape
    flat = (peers * slots, HEAD_SIZE)
    mine = keep_ref[:, KEY_VALUE_HEADS].reshape(flat)
    theirs = came_ref[:, KEY_VALUE_HEADS].astype(F32).reshape(flat)
    lane = lax.broadcasted_iota(jnp.int32, flat, 1)
    state = jnp.zeros(flat, F32)
    for g in range(KEY_VALUE_HEADS):
        my_peak, my_total = state_columns(mine, g)
        their_peak, their_total = state_columns(theirs, g)
        peak = jnp.maximum(my_peak, their_peak)
        my_scale, their_scale = jnp.exp(my_peak - peak), jnp.exp(their_peak - peak)
        total = my_total * my_scale + their_total * their_scale
        summed = (
            keep_ref[:, g].reshape(flat) * my_scale
            + came_ref[:, g].astype(F32).reshape(flat) * their_scale
        )
        total_high = rounded(total)
        for index, column in enumerate((peak, total_high, total - total_high)):
            state = jnp.where(lane == index * KEY_VALUE_HEADS + g, column, state)
        out_ref[:, g] = summed.astype(BF16).reshape(peers, slots, HEAD_SIZE)
    out_ref[:, KEY_VALUE_HEADS] = state.astype(BF16).reshape(peers, slots, HEAD_SIZE)


def merge(keep, came):
    return pl.pallas_call(
        merge_kernel,
        out_shape=pltpu.VMEM(came.shape, BF16),
        in_specs=[VMEM, VMEM],
        out_specs=VMEM,
        compiler_params=pltpu.CompilerParams(vmem_limit_bytes=8 * MIB),
        name="merge",
    )(in_vmem(keep), in_vmem(came))


def finish_kernel(parts_ref, gain_ref, out_ref, row_ref):
    peers, _, slots, _ = parts_ref.shape
    rows = slots // GROUP
    state = parts_ref[:, KEY_VALUE_HEADS].astype(F32)
    scale = jnp.exp(state - jnp.max(state, axis=0, keepdims=True))
    attended = []
    squares = jnp.zeros((slots, HEAD_SIZE), F32)
    for g in range(KEY_VALUE_HEADS):
        summed = jnp.zeros((slots, HEAD_SIZE), F32)
        total = jnp.zeros((slots, 1), F32)
        for peer in range(peers):
            by = scale[peer][:, g : g + 1]
            summed += parts_ref[peer, g].astype(F32) * by
            total += state_columns(state[peer], g)[1] * by
        one = rounded(summed / total)
        squares += one * one
        attended.append(one)
    mean_square = (
        jnp.sum(squares.reshape(rows, GROUP, HEAD_SIZE), axis=(1, 2), keepdims=True) / D + 1e-05
    )
    inverse = lax.rsqrt(mean_square)
    for g in range(KEY_VALUE_HEADS):
        normed = attended[g].reshape(rows, GROUP, HEAD_SIZE) * inverse * gain_ref[g][None]
        for row in range(rows):
            for head in range(GROUP):
                start = (g * GROUP + head) * HEAD_SIZE
                row_ref[row : row + 1, start : start + HEAD_SIZE] = normed[row, head : head + 1]
    packed = row_ref[...].astype(BF16)
    for peer in range(peers):
        out_ref[peer] = packed


def finish(parts, norm_gain):
    peers, _, slots, _ = parts.shape
    rows = slots // GROUP
    return pl.pallas_call(
        finish_kernel,
        out_shape=pltpu.VMEM((peers, rows, D), BF16),
        in_specs=[VMEM, VMEM],
        out_specs=VMEM,
        scratch_shapes=[pltpu.VMEM((rows, D), F32)],
        compiler_params=pltpu.CompilerParams(vmem_limit_bytes=8 * MIB),
        name="finish",
    )(in_vmem(parts), norm_gain.reshape(KEY_VALUE_HEADS, GROUP, HEAD_SIZE))


def feed_forward_kernel(
    near_ref, far_ref, gate_ref, up_hbm, down_hbm, keep_ref, send_ref, x_ref, up_ref, down_ref, sems,
    *, chunks,
):
    half, width = near_ref.shape
    step = width // chunks

    def copies(source, target, base):
        return [
            pltpu.make_async_copy(
                source.at[:, pl.ds(i * step, step)], target.at[:, pl.ds(i * step, step)], sems.at[base + i]
            )
            for i in range(chunks)
        ]

    ups, downs = copies(up_hbm, up_ref, 0), copies(down_hbm, down_ref, chunks)
    for copy in ups + downs:
        copy.start()
    x_ref[:half] = near_ref[...]
    x_ref[half:] = far_ref[...]
    hidden = gate_ref.shape[0]
    gate = lax.dot_general(x_ref[...], gate_ref[...], ROWS_BY_ROWS, preferred_element_type=F32)
    gate = gate / (1.0 + jnp.exp(-gate))
    upward = jnp.zeros((2 * half, hidden), F32)
    for i, copy in enumerate(ups):
        copy.wait()
        part = slice(i * step, (i + 1) * step)
        upward += lax.dot_general(
            x_ref[:, part], up_ref[:, part], ROWS_BY_ROWS, preferred_element_type=F32
        )
    activated = (gate * upward).astype(BF16)
    for i, copy in enumerate(downs):
        copy.wait()
        part = slice(i * step, (i + 1) * step)
        out = jnp.dot(activated, down_ref[:, part], preferred_element_type=F32)
        keep_ref[:, part] = out[:half]
        send_ref[:, part] = out[half:].astype(BF16)


def feed_forward(near, far, gate, up, down):
    half, width = near.shape
    chunks = 8
    return pl.pallas_call(
        functools.partial(feed_forward_kernel, chunks=chunks),
        out_shape=(pltpu.VMEM(near.shape, F32), pltpu.VMEM(near.shape, BF16)),
        in_specs=[VMEM, VMEM, VMEM, ANY, ANY],
        out_specs=(VMEM, VMEM),
        scratch_shapes=[
            pltpu.VMEM((2 * half, width), BF16),
            pltpu.VMEM(up.shape, up.dtype),
            pltpu.VMEM(down.shape, down.dtype),
            pltpu.SemaphoreType.DMA((2 * chunks,)),
        ],
        compiler_params=pltpu.CompilerParams(vmem_limit_bytes=40 * MIB),
        cost_estimate=pl.CostEstimate(
            flops=12 * half * gate.size, bytes_accessed=4 * up.size, transcendentals=half * up.shape[0]
        ),
        name="feed_forward",
    )(in_vmem(near), in_vmem(far), in_vmem(gate), up, down)


def stacked(blocks):
    peers, rows, _ = blocks.shape
    out = None
    for i in range(peers):
        edges = ((i * rows, (peers - 1 - i) * rows, 0), (0, 0, 0))
        placed = lax.pad(blocks[i], jnp.array(-jnp.inf, blocks.dtype), edges)
        out = placed if out is None else jnp.maximum(out, placed)
    return out


def local(
    queries,
    cached_key_rows,
    cached_value_rows,
    cache_position,
    lengths,
    norm_gain,
    gate_weight,
    up_weight,
    down_weight,
):
    devices = lax.axis_size("ctx")
    peers = devices // 2
    rows = queries.shape[0]
    same_core = [[2 * i + core for i in range(peers)] for core in range(2)]
    partners = [(i, i ^ 1) for i in range(devices)]

    def exchange(x):
        return lax.all_to_all(x, "ctx", 0, 0, axis_index_groups=same_core, tiled=True)

    def swap(x):
        return lax.ppermute(x, "ctx", partners)

    near = exchange(pack(queries, lengths, peers))
    keep, send, gate = attend(
        near, swap(near), cache_position.reshape(1, -1), cached_key_rows, cached_value_rows, gate_weight
    )
    parts = exchange(merge(keep, swap(send)))
    near = stacked(exchange(finish(parts, norm_gain)))
    keep, send = feed_forward(near, swap(near), gate, up_weight, down_weight)
    shares = (keep + swap(send).astype(F32)).astype(BF16)
    shares = exchange(shares.reshape(peers, rows, D))
    return jnp.sum(shares.astype(F32), axis=0).astype(BF16)


def solution(mesh):
    placed = (
        P(("groups", "ctx"), None),
        P(("groups", "ctx"), None),
        P(("groups", "ctx"), None),
        P(("groups", "ctx")),
        P(("groups", "ctx")),
        P(),
        P("ctx", None),
        P("ctx", None),
        P("ctx", None),
    )
    return jax.shard_map(
        local, mesh=mesh, in_specs=placed, out_specs=P(("groups", "ctx"), None), check_vma=False
    )
```

time: 215 us -> 99.7 us (0.46)
  blocking collectives: 136 us -> 54.9 us
  matrix products: 26.6 us -> 0 us
  Pallas kernels: 0 us -> 26.5 us
  waiting for transfers between devices: 26.3 us -> 5.95 us
  starting transfers between devices: 7.12 us -> 0.47 us
  other arithmetic: 5.16 us -> 1.28 us
    unnamed x2 -> x0, blocking collectives: 83.3 us -> none
    all_to_all x1 -> x4, blocking collectives: 8.99 us -> 54.9 us  [exchange(): lax.all_to_all(x, 'ctx', 0, 0, axis_index_groups=same_core, tiled=True)]
    all_gather x2 -> x0, blocking collectives: 43.6 us -> none  [the longest x1 24 us: local(): piece = lax.all_gather(normed, 'ctx', axis=0, tiled=True)]
    dot_general x6 -> x0, matrix products: 26.6 us -> none  [the longest x1 14.1 us: local(): jnp.dot(activated, down_weight, preferred_element_type=jnp.float32)]
    pallas_call x0 -> x5, Pallas kernels: none -> 26.5 us  [the longest x1 20.4 us: feed_forward(): pl.pallas_call(functools.partial(feed_forward_kernel, chunks=chunks), out...]
    all_to_all x2 -> x0, waiting for transfers between devices: 26.3 us -> none  [the longest x1 20.1 us: local(): lax.all_to_all(summed_all, 'ctx', split_axis=0, concat_axis=0, tiled=True)]
    all_to_all x2 -> x0, starting transfers between devices: 7.12 us -> none  [the longest x1 3.65 us: local(): lax.all_to_all(summed_all, 'ctx', split_axis=0, concat_axis=0, tiled=True)]
    unnamed x10 -> x14, local copies, waits for them, and re-layouts: 3.41 us -> 9.72 us
  transfers between devices with their start and end apart: 2 -> 4, of which waited for: 2 -> 4; matrix products, arithmetic and copies ran while one was open for 1% -> 0% of each run, Pallas kernels for 0% -> 0%
where the time goes in v1:
time: 99.7 us; the launch traced here: 99.2 us
  blocking collectives  54.9 us (55%)
  Pallas kernels  26.5 us (27%)
  local copies, waits for them, and re-layouts  10.1 us (10%)
  waiting for transfers between devices  5.95 us (6%)
  other arithmetic  1.28 us (1%)
    all_to_all x4, blocking collectives, exchange(): lax.all_to_all(x, 'ctx', 0, 0, axis_index_groups=same_core, tiled=True)  54.9 us
    pallas_call x1, Pallas kernels, feed_forward(): pl.pallas_call(functools.partial(feed_forward_kernel, chunks=chunks), out...  20.4 us
    unnamed x14, local copies, waits for them, and re-layouts  9.72 us
    ppermute x4, waiting for transfers between devices, swap(): return lax.ppermute(x, 'ctx', partners)  5.95 us
    pallas_call x1, Pallas kernels, attend(): pl.pallas_call(attend_kernel, out_shape=(pltpu.VMEM(near.shape, F32), plt...  4.28 us
  transfers between devices with their start and end apart: 4, of which 4 were waited for; matrix products, arithmetic and copies ran while one was open for 0% of the time, Pallas kernels for 0%

profile of v1, /device:TPU:0, one launch (start us, length us, event | category | flops | bytes accessed | tf_op | source)
XLA Modules:
  0.0 99.2 jit_solution(5806078787573101333)
XLA Ops:
  0.0 0.0 copy-start.3
  0.0 0.8 copy-done.3
  0.8 0.0 copy-start.6
  0.8 0.7 copy-done.6
  1.4 0.0 copy-start.4
  1.4 0.6 pack.1
  2.0 17.4 %all_to_all.20.near_ref = bf16[8,9,16,128]{3,2,1,0:T(8,128)(2,1)S(1)} all-to-all(bf16[8,9,16,128]{3,2,1,0:T(8,128)(2,1)S(1)} %pack.1), channel_id=1, replica_groups={{0,2,4,6,8,10,12,14},{1,3,5,7,9,11,13,15},{16,18,20,22,24,26,28,30},{17..., dimensions={0} | all-to-all | bytes 589824 | tf_op jit(solution)/shard_map/all_to_all | solution.py:312
  19.5 0.0 collective-permute-start
  19.5 1.6 %collective-permute-done.far_ref = bf16[8,9,16,128]{3,2,1,0:T(8,128)(2,1)S(1)} collective-permute-done((bf16[8,9,16,128]{3,2,1,0:T(8,128)(2,1)S(1)}, bf16[8,9,16,128]{3,2,1,0:T(8,128)(2,1)S(1)}, u32[]{:S(2)}, u32[]{:S(2)}) %collective-permute-start) | collective-permute-done | bytes 294944 | tf_op jit(solution)/shard_map/ppermute | solution.py:315
  21.1 0.0 copy-start
  21.1 5.2 %copy-done = bf16[896,8192]{1,0:T(8,128)(2,1)S(1)} copy-done((bf16[896,8192]{1,0:T(8,128)(2,1)S(1)}, bf16[896,8192]{1,0:T(8,128)(2,1)}, u32[]{:S(2)}) %copy-start) | copy-done | bytes 14680088
  26.2 1.2 %copy-done.1 = bf16[512,1024]{1,0:T(8,128)(2,1)S(1)} copy-done((bf16[512,1024]{1,0:T(8,128)(2,1)S(1)}, bf16[512,1024]{1,0:T(8,128)(2,1)}, u32[]{:S(2)}) %copy-start.1) | copy-done | bytes 1048600
  27.5 1.2 %copy-done.2 = bf16[512,1024]{1,0:T(8,128)(2,1)S(1)} copy-done((bf16[512,1024]{1,0:T(8,128)(2,1)S(1)}, bf16[512,1024]{1,0:T(8,128)(2,1)}, u32[]{:S(2)}) %copy-start.2) | copy-done | bytes 1048600
  28.7 0.7 copy-done.5
  29.4 4.3 %attend.1 = (f32[8,9,16,128]{3,2,1,0:T(8,128)S(1)}, bf16[8,9,16,128]{3,2,1,0:T(8,128)(2,1)S(1)}, bf16[896,8192]{1,0:T(8,128)(2,1)S(1)}) custom-call(bf16[8,9,16,128]{3,2,1,0:T(8,128)(2,1)S(1)} %all_to_all.20.near_ref, bf16[8,9,16,128]{3,2,1,0:T(8,128)(2,1)S(1)} %collective-permute-done.far_ref, s32[1,512]{1,0:T(1,128)S(1)} %bitcast.19, ...), custom_call_target="tpu_custom_call" | custom-call | flops 603979776 | bytes 14680064 | tf_op jit(solution)/shard_map/attend/pallas_call | solution.py:113
  33.6 0.2 collective-permute-start.1
  33.8 1.5 %collective-permute-done.1.came_ref = bf16[8,9,16,128]{3,2,1,0:T(8,128)(2,1)S(1)} collective-permute-done((bf16[8,9,16,128]{3,2,1,0:T(8,128)(2,1)S(1)}, bf16[8,9,16,128]{3,2,1,0:T(8,128)(2,1)S(1)}, u32[]{:S(2)}, u32[]{:S(2)}) %collective-permute-start.1) | collective-permute-done | bytes 294944 | tf_op jit(solution)/shard_map/ppermute | solution.py:315
  35.3 0.6 merge.1
  35.9 13.3 %all_to_all.21.parts_ref = bf16[8,9,16,128]{3,2,1,0:T(8,128)(2,1)S(1)} all-to-all(bf16[8,9,16,128]{3,2,1,0:T(8,128)(2,1)S(1)} %merge.1), channel_id=1, replica_groups={{0,2,4,6,8,10,12,14},{1,3,5,7,9,11,13,15},{16,18,20,22,24,26,28,30},{17..., dimensions={0} | all-to-all | bytes 589824 | tf_op jit(solution)/shard_map/all_to_all | solution.py:312
  49.3 0.0 copy-done.4
  49.3 0.5 finish.1
  49.8 11.5 %all_to_all.22 = bf16[8,2,8192]{2,1,0:T(2,128)(2,1)S(1)} all-to-all(bf16[8,2,8192]{2,1,0:T(2,128)(2,1)S(1)} %finish.1), channel_id=1, replica_groups={{0,2,4,6,8,10,12,14},{1,3,5,7,9,11,13,15},{16,18,20,22,24,26,28,30},{17..., dimensions={0} | all-to-all | bytes 524288 | tf_op jit(solution)/shard_map/all_to_all | solution.py:312
  61.3 0.2 slice_bitcast_fusion.7
  61.5 0.4 pad_maximum_fusion.near_ref
  61.8 0.1 collective-permute-start.2
  61.9 1.5 %collective-permute-done.2.far_ref = bf16[16,8192]{1,0:T(8,128)(2,1)S(1)} collective-permute-done((bf16[16,8192]{1,0:T(8,128)(2,1)S(1)}, bf16[16,8192]{1,0:T(8,128)(2,1)S(1)}, u32[]{:S(2)}, u32[]{:S(2)}) %collective-permute-start.2) | collective-permute-done | bytes 262176 | tf_op jit(solution)/shard_map/ppermute | solution.py:315
  63.4 20.4 %feed_forward.1 = (f32[16,8192]{1,0:T(8,128)S(1)}, bf16[16,8192]{1,0:T(8,128)(2,1)S(1)}) custom-call(bf16[16,8192]{1,0:T(8,128)(2,1)S(1)} %pad_maximum_fusion.near_ref, bf16[16,8192]{1,0:T(8,128)(2,1)S(1)} %collective-permute-done.2.far_ref, bf16[896,8192]{1,0:T(8,128)(2,1)S(1)} %get-tuple-element.12.gate_ref, bf16[896,8192]{1,0:T(8,128)(2,1)} %up_hbm.1, ...), custom_call_target="tpu_custom_call" | custom-call | flops 1409286144 | bytes 29360128 | tf_op jit(solution)/shard_map/feed_forward/pallas_call | solution.py:265
  83.9 0.2 collective-permute-start.3
  84.1 1.4 %collective-permute-done.3 = bf16[16,8192]{1,0:T(8,128)(2,1)S(1)} collective-permute-done((bf16[16,8192]{1,0:T(8,128)(2,1)S(1)}, bf16[16,8192]{1,0:T(8,128)(2,1)S(1)}, u32[]{:S(2)}, u32[]{:S(2)}) %collective-permute-start.3) | collective-permute-done | bytes 262176 | tf_op jit(solution)/shard_map/ppermute | solution.py:315
  85.5 0.2 reshape.11
  85.7 12.6 %all_to_all.23 = bf16[8,2,8192]{2,1,0:T(2,128)(2,1)S(1)} all-to-all(bf16[8,2,8192]{2,1,0:T(2,128)(2,1)S(1)} %reshape.11), channel_id=1, replica_groups={{0,2,4,6,8,10,12,14},{1,3,5,7,9,11,13,15},{16,18,20,22,24,26,28,30},{17..., dimensions={0} | all-to-all | bytes 524288 | tf_op jit(solution)/shard_map/all_to_all | solution.py:312
  98.3 0.9 reduce_sum.12
  (4 shorter events, 0.1 us)
Async XLA Ops:
  0.0 0.8 copy-start.3
  0.8 0.7 copy-start.6
  1.4 47.8 %copy-start.4 = (f32[8192]{0:T(1024)S(1)}, f32[8192]{0:T(1024)}, u32[]{:S(2)}) copy-start(f32[8192]{0:T(1024)} %param.14) | copy-start | bytes 98308
  19.5 1.6 %collective-permute-start = (bf16[8,9,16,128]{3,2,1,0:T(8,128)(2,1)S(1)}, bf16[8,9,16,128]{3,2,1,0:T(8,128)(2,1)S(1)}, u32[]{:S(2)}, u32[]{:S(2)}) collective-permute-start(bf16[8,9,16,128]{3,2,1,0:T(8,128)(2,1)S(1)} %all_to_all.20.near_ref), channel_id=1, source_target_pairs={{0,1},{1,0},{2,3},{3,2},{4,5},{5,4},{6,7},{7,6},{8,9},{9,8},{10,11... | collective-permute-start | bytes 884744 | tf_op jit(solution)/shard_map/ppermute | solution.py:315
  21.1 5.2 %copy-start = (bf16[896,8192]{1,0:T(8,128)(2,1)S(1)}, bf16[896,8192]{1,0:T(8,128)(2,1)}, u32[]{:S(2)}) copy-start(bf16[896,8192]{1,0:T(8,128)(2,1)} %w_hbm.1) | copy-start | bytes 44040196
  26.2 1.2 %copy-start.1 = (bf16[512,1024]{1,0:T(8,128)(2,1)S(1)}, bf16[512,1024]{1,0:T(8,128)(2,1)}, u32[]{:S(2)}) copy-start(bf16[512,1024]{1,0:T(8,128)(2,1)} %k_hbm.1) | copy-start | bytes 3145732
  27.5 1.2 %copy-start.2 = (bf16[512,1024]{1,0:T(8,128)(2,1)S(1)}, bf16[512,1024]{1,0:T(8,128)(2,1)}, u32[]{:S(2)}) copy-start(bf16[512,1024]{1,0:T(8,128)(2,1)} %v_hbm.1) | copy-start | bytes 3145732
  28.7 0.7 copy-start.5
  33.6 1.6 %collective-permute-start.1 = (bf16[8,9,16,128]{3,2,1,0:T(8,128)(2,1)S(1)}, bf16[8,9,16,128]{3,2,1,0:T(8,128)(2,1)S(1)}, u32[]{:S(2)}, u32[]{:S(2)}) collective-permute-start(bf16[8,9,16,128]{3,2,1,0:T(8,128)(2,1)S(1)} %get-tuple-element.11), channel_id=1, source_target_pairs={{0,1},{1,0},{2,3},{3,2},{4,5},{5,4},{6,7},{7,6},{8,9},{9,8},{10,11... | collective-permute-start | bytes 884744 | tf_op jit(solution)/shard_map/ppermute | solution.py:315
  61.8 1.6 %collective-permute-start.2 = (bf16[16,8192]{1,0:T(8,128)(2,1)S(1)}, bf16[16,8192]{1,0:T(8,128)(2,1)S(1)}, u32[]{:S(2)}, u32[]{:S(2)}) collective-permute-start(bf16[16,8192]{1,0:T(8,128)(2,1)S(1)} %pad_maximum_fusion.near_ref), channel_id=1, source_target_pairs={{0,1},{1,0},{2,3},{3,2},{4,5},{5,4},{6,7},{7,6},{8,9},{9,8},{10,11... | collective-permute-start | bytes 786440 | tf_op jit(solution)/shard_map/ppermute | solution.py:315
  83.9 1.6 %collective-permute-start.3 = (bf16[16,8192]{1,0:T(8,128)(2,1)S(1)}, bf16[16,8192]{1,0:T(8,128)(2,1)S(1)}, u32[]{:S(2)}, u32[]{:S(2)}) collective-permute-start(bf16[16,8192]{1,0:T(8,128)(2,1)S(1)} %get-tuple-element.14), channel_id=1, source_target_pairs={{0,1},{1,0},{2,3},{3,2},{4,5},{5,4},{6,7},{7,6},{8,9},{9,8},{10,11... | collective-permute-start | bytes 786440 | tf_op jit(solution)/shard_map/ppermute | solution.py:315

commit v2 on v1

--- a/solution.py
+++ b/solution.py
@@ -16,7 +16,6 @@
 BF16 = jnp.bfloat16
 ROWS_BY_ROWS = (((1,), (1,)), ((), ()))
 VMEM = pl.BlockSpec(memory_space=pltpu.VMEM)
-SMEM = pl.BlockSpec(memory_space=pltpu.SMEM)
 ANY = pl.BlockSpec(memory_space=pl.ANY)
 MIB = 1 << 20
 
@@ -25,12 +24,24 @@
     return pltpu.with_memory_space_constraint(x, pltpu.VMEM)
 
 
+def in_hbm(x):
+    return pltpu.with_memory_space_constraint(x, pltpu.HBM)
+
+
 def rounded(x):
     return x.astype(BF16).astype(F32)
 
 
-def pack_kernel(lengths_ref, q_ref, out_ref, slab_ref):
+def pack_kernel(lengths_hbm, q_hbm, out_ref, slab_ref, lengths_ref, q_ref, sems):
     rows = q_ref.shape[0]
+    copies = (
+        pltpu.make_async_copy(q_hbm, q_ref, sems.at[0]),
+        pltpu.make_async_copy(lengths_hbm, lengths_ref, sems.at[1]),
+    )
+    for copy in copies:
+        copy.start()
+    for copy in copies:
+        copy.wait()
     q = q_ref[...].astype(F32)
     lane = lax.broadcasted_iota(jnp.int32, (GROUP, HEAD_SIZE), 1)
     for row in range(rows):
@@ -55,24 +66,54 @@
     return pl.pallas_call(
         pack_kernel,
         out_shape=pltpu.VMEM((peers,) + shape, BF16),
-        in_specs=[SMEM, VMEM],
+        in_specs=[ANY, ANY],
         out_specs=VMEM,
-        scratch_shapes=[pltpu.VMEM(shape, F32)],
+        scratch_shapes=[
+            pltpu.VMEM(shape, F32),
+            pltpu.SMEM(lengths.shape, lengths.dtype),
+            pltpu.VMEM(queries.shape, queries.dtype),
+            pltpu.SemaphoreType.DMA((2,)),
+        ],
         compiler_params=pltpu.CompilerParams(vmem_limit_bytes=4 * MIB),
         name="pack",
-    )(lengths, queries)
-
-
-def attend_kernel(
-    near_ref, far_ref, position_ref, k_hbm, v_hbm, w_hbm,
-    keep_ref, send_ref, w_ref, k_ref, v_ref, sems,
-):
+    )(in_hbm(lengths), in_hbm(queries))
+
+
+def load_kernel(*refs, starts):
+    count = len(starts)
     copies = [
-        pltpu.make_async_copy(source, target, sems.at[i])
-        for i, (source, target) in enumerate(((k_hbm, k_ref), (v_hbm, v_ref), (w_hbm, w_ref)))
+        pltpu.make_async_copy(
+            refs[i].at[pl.ds(start, refs[count + i].shape[0])], refs[count + i], refs[-1].at[i]
+        )
+        for i, start in enumerate(starts)
     ]
     for copy in copies:
         copy.start()
+    for copy in copies:
+        copy.wait()
+
+
+def load(*entries):
+    shapes = [((a.shape[0] - start,) + a.shape[1:], a.dtype) for a, start in entries]
+    return pl.pallas_call(
+        functools.partial(load_kernel, starts=tuple(start for _, start in entries)),
+        out_shape=tuple(pltpu.VMEM(*shape) for shape in shapes),
+        in_specs=[ANY] * len(entries),
+        out_specs=(VMEM,) * len(entries),
+        scratch_shapes=[pltpu.SemaphoreType.DMA((len(entries),))],
+        compiler_params=pltpu.CompilerParams(vmem_limit_bytes=MIB),
+        cost_estimate=pl.CostEstimate(
+            flops=0, bytes_accessed=sum(4 * a.size for a, _ in entries), transcendentals=0
+        ),
+        name="load",
+    )(*(in_hbm(a) for a, _ in entries))
+
+
+def attend_kernel(
+    near_ref, far_ref, position_ref, k_ref, v_ref, w_hbm, keep_ref, send_ref, w_ref, sem
+):
+    copy = pltpu.make_async_copy(w_hbm.at[pl.ds(0, w_ref.shape[0])], w_ref, sem)
+    copy.start()
     peers, _, slots, _ = near_ref.shape
     half = peers * slots
 
@@ -86,8 +127,6 @@
     live = position_ref[...].astype(F32) < lengths
     lane = lax.broadcasted_iota(jnp.int32, (2 * half, HEAD_SIZE), 1)
     state = jnp.zeros((2 * half, HEAD_SIZE), F32)
-    copies[0].wait()
-    copies[1].wait()
     for g in range(KEY_VALUE_HEADS):
         columns = slice(g * HEAD_SIZE, (g + 1) * HEAD_SIZE)
         scores = lax.dot_general(
@@ -105,31 +144,27 @@
         send_ref[:, g] = summed[half:].astype(BF16).reshape(peers, slots, HEAD_SIZE)
     keep_ref[:, KEY_VALUE_HEADS] = state[:half].reshape(peers, slots, HEAD_SIZE)
     send_ref[:, KEY_VALUE_HEADS] = state[half:].astype(BF16).reshape(peers, slots, HEAD_SIZE)
-    copies[2].wait()
-
-
-def attend(near, far, position, keys, values, weight):
+    copy.wait()
+
+
+def attend(near, far, position, keys, values, weight, weight_rows):
     cells = near.size // HEAD_SIZE * keys.shape[0]
     return pl.pallas_call(
         attend_kernel,
         out_shape=(
             pltpu.VMEM(near.shape, F32),
             pltpu.VMEM(near.shape, BF16),
-            pltpu.VMEM(weight.shape, weight.dtype),
+            pltpu.VMEM((weight_rows, weight.shape[1]), weight.dtype),
         ),
-        in_specs=[VMEM, VMEM, VMEM, ANY, ANY, ANY],
-        out_specs=(VMEM, VMEM, VMEM),
-        scratch_shapes=[
-            pltpu.VMEM(keys.shape, keys.dtype),
-            pltpu.VMEM(values.shape, values.dtype),
-            pltpu.SemaphoreType.DMA((3,)),
-        ],
-        compiler_params=pltpu.CompilerParams(vmem_limit_bytes=20 * MIB),
+        in_specs=[VMEM] * 5 + [ANY],
+        out_specs=(VMEM,) * 3,
+        scratch_shapes=[pltpu.SemaphoreType.DMA],
+        compiler_params=pltpu.CompilerParams(vmem_limit_bytes=12 * MIB + 16 * near.size),
         cost_estimate=pl.CostEstimate(
-            flops=8 * cells * HEAD_SIZE, bytes_accessed=2 * weight.size, transcendentals=2 * cells
+            flops=8 * cells * HEAD_SIZE, bytes_accessed=4 * keys.size, transcendentals=2 * cells
         ),
         name="attend",
-    )(in_vmem(near), in_vmem(far), position, keys, values, weight)
+    )(*(in_vmem(x) for x in (near, far, position, keys, values)), in_hbm(weight))
 
 
 def state_columns(state, g):
@@ -221,64 +256,71 @@
 
 
 def feed_forward_kernel(
-    near_ref, far_ref, gate_ref, up_hbm, down_hbm, keep_ref, send_ref, x_ref, up_ref, down_ref, sems,
-    *, chunks,
+    near_ref, far_ref, gate_a_ref, gate_b_ref, up_hbm, down_hbm, keep_ref, send_ref,
+    x_ref, up_ref, down_ref, up_sems, down_sems,
 ):
     half, width = near_ref.shape
-    step = width // chunks
-
-    def copies(source, target, base):
-        return [
-            pltpu.make_async_copy(
-                source.at[:, pl.ds(i * step, step)], target.at[:, pl.ds(i * step, step)], sems.at[base + i]
-            )
-            for i in range(chunks)
-        ]
-
-    ups, downs = copies(up_hbm, up_ref, 0), copies(down_hbm, down_ref, chunks)
-    for copy in ups + downs:
-        copy.start()
+    ups, downs = up_sems.shape[0], down_sems.shape[0]
+    depth, step = up_ref.shape[0] // ups, width // downs
+    up_parts = [pl.ds(i * depth, depth) for i in range(ups)]
+    down_parts = [pl.ds(i * step, step) for i in range(downs)]
+    up_copies = [
+        pltpu.make_async_copy(up_hbm.at[part], up_ref.at[part], up_sems.at[i])
+        for i, part in enumerate(up_parts)
+    ]
+    down_copies = [
+        pltpu.make_async_copy(down_hbm.at[:, part], down_ref.at[:, part], down_sems.at[i])
+        for i, part in enumerate(down_parts)
+    ]
+
+    up_copies[0].start()
     x_ref[:half] = near_ref[...]
     x_ref[half:] = far_ref[...]
-    hidden = gate_ref.shape[0]
-    gate = lax.dot_general(x_ref[...], gate_ref[...], ROWS_BY_ROWS, preferred_element_type=F32)
-    gate = gate / (1.0 + jnp.exp(-gate))
-    upward = jnp.zeros((2 * half, hidden), F32)
-    for i, copy in enumerate(ups):
-        copy.wait()
-        part = slice(i * step, (i + 1) * step)
-        upward += lax.dot_general(
-            x_ref[:, part], up_ref[:, part], ROWS_BY_ROWS, preferred_element_type=F32
-        )
-    activated = (gate * upward).astype(BF16)
-    for i, copy in enumerate(downs):
-        copy.wait()
-        part = slice(i * step, (i + 1) * step)
-        out = jnp.dot(activated, down_ref[:, part], preferred_element_type=F32)
-        keep_ref[:, part] = out[:half]
-        send_ref[:, part] = out[half:].astype(BF16)
-
-
-def feed_forward(near, far, gate, up, down):
+    x = x_ref[...]
+
+    def project(weight):
+        return lax.dot_general(x, weight, ROWS_BY_ROWS, preferred_element_type=F32)
+
+    gate_a = project(gate_a_ref[...])
+    up_copies[1].start()
+    gate = jnp.concatenate([gate_a, project(gate_b_ref[...])], axis=1)
+    upward = []
+    for i in range(ups):
+        up_copies[i].wait()
+        down_copies[i].start()
+        upward.append(project(up_ref[i * depth : (i + 1) * depth]))
+    upward = jnp.concatenate(upward, axis=1)
+    activated = (gate / (1.0 + jnp.exp(-gate)) * upward).astype(BF16)
+    for i in range(downs):
+        if i + ups < downs:
+            down_copies[i + ups].start()
+        down_copies[i].wait()
+        out = jnp.dot(activated, down_ref[:, down_parts[i]], preferred_element_type=F32)
+        keep_ref[:, down_parts[i]] = out[:half]
+        send_ref[:, down_parts[i]] = out[half:].astype(BF16)
+
+
+def feed_forward(near, far, gate_a, gate_b, up, down):
     half, width = near.shape
-    chunks = 8
-    return pl.pallas_call(
-        functools.partial(feed_forward_kernel, chunks=chunks),
+    ups, downs = 2, 4
+    return pl.pallas_call(
+        feed_forward_kernel,
         out_shape=(pltpu.VMEM(near.shape, F32), pltpu.VMEM(near.shape, BF16)),
-        in_specs=[VMEM, VMEM, VMEM, ANY, ANY],
+        in_specs=[VMEM] * 4 + [ANY, ANY],
         out_specs=(VMEM, VMEM),
         scratch_shapes=[
             pltpu.VMEM((2 * half, width), BF16),
             pltpu.VMEM(up.shape, up.dtype),
             pltpu.VMEM(down.shape, down.dtype),
-            pltpu.SemaphoreType.DMA((2 * chunks,)),
+            pltpu.SemaphoreType.DMA((ups,)),
+            pltpu.SemaphoreType.DMA((downs,)),
         ],
-        compiler_params=pltpu.CompilerParams(vmem_limit_bytes=40 * MIB),
+        compiler_params=pltpu.CompilerParams(vmem_limit_bytes=36 * MIB),
         cost_estimate=pl.CostEstimate(
-            flops=12 * half * gate.size, bytes_accessed=4 * up.size, transcendentals=half * up.shape[0]
+            flops=12 * half * up.size, bytes_accessed=4 * down.size, transcendentals=half * up.shape[0]
         ),
         name="feed_forward",
-    )(in_vmem(near), in_vmem(far), in_vmem(gate), up, down)
+    )(*(in_vmem(x) for x in (near, far, gate_a, gate_b)), in_hbm(up), in_hbm(down))
 
 
 def stacked(blocks):
@@ -305,7 +347,8 @@
     devices = lax.axis_size("ctx")
     peers = devices // 2
     rows = queries.shape[0]
-    same_core = [[2 * i + core for i in range(peers)] for core in range(2)]
+    around = [*range(0, peers, 2), *reversed(range(1, peers, 2))]
+    same_core = [[2 * i + core for i in around] for core in range(2)]
     partners = [(i, i ^ 1) for i in range(devices)]
 
     def exchange(x):
@@ -315,12 +358,19 @@
         return lax.ppermute(x, "ctx", partners)
 
     near = exchange(pack(queries, lengths, peers))
-    keep, send, gate = attend(
-        near, swap(near), cache_position.reshape(1, -1), cached_key_rows, cached_value_rows, gate_weight
-    )
-    parts = exchange(merge(keep, swap(send)))
+    first_rows = gate_weight.shape[0] * 6 // 7
+    late_keys, near = lax.optimization_barrier((cached_key_rows, near))
+    far = swap(near)
+    keys, values, position = load(
+        (late_keys, 0), (cached_value_rows, 0), (cache_position.reshape(1, -1), 0)
+    )
+    keep, send, gate_a = attend(near, far, position, keys, values, gate_weight, first_rows)
+    late_gate, send = lax.optimization_barrier((gate_weight, send))
+    came = swap(send)
+    (gate_b,) = load((late_gate, first_rows))
+    parts = exchange(merge(keep, came))
     near = stacked(exchange(finish(parts, norm_gain)))
-    keep, send = feed_forward(near, swap(near), gate, up_weight, down_weight)
+    keep, send = feed_forward(near, swap(near), gate_a, gate_b, up_weight, down_weight)
     shares = (keep + swap(send).astype(F32)).astype(BF16)
     shares = exchange(shares.reshape(peers, rows, D))
     return jnp.sum(shares.astype(F32), axis=0).astype(BF16)

time: 99.7 us -> 83.8 us (0.84)
  local copies, waits for them, and re-layouts: 10.1 us -> 0.37 us
  Pallas kernels: 26.5 us -> 22.9 us
  waiting for transfers between devices: 5.95 us -> 2.38 us
    unnamed x14 -> x2, local copies, waits for them, and re-layouts: 9.72 us -> 0.01 us
    pallas_call x1 -> x3, Pallas kernels: 20.4 us -> 16.3 us  [the longest x1 13.1 us: feed_forward(): pl.pallas_call(feed_forward_kernel, out_shape=(pltpu.VMEM(near.shape, F32...]
    ppermute x4, waiting for transfers between devices: 5.95 us -> 2.38 us  [swap(): return lax.ppermute(x, 'ctx', partners)]
  transfers between devices with their start and end apart: 4 -> 4, of which waited for: 4 -> 2; matrix products, arithmetic and copies ran while one was open for 0% -> 0% of each run, Pallas kernels for 0% -> 4%
where the time goes in v2:
time: 83.8 us; the launch traced here: 83.3 us
  blocking collectives  55.1 us (66%)
  Pallas kernels  22.9 us (27%)
  waiting for transfers between devices  2.38 us (3%)
  other arithmetic  1.28 us (2%)
  starting transfers between devices  1.2 us (1%)
    all_to_all x4, blocking collectives, exchange(): lax.all_to_all(x, 'ctx', 0, 0, axis_index_groups=same_core, tiled=True)  55.1 us
    pallas_call x1, Pallas kernels, feed_forward(): pl.pallas_call(feed_forward_kernel, out_shape=(pltpu.VMEM(near.shape, F32...  13.1 us
    pallas_call x1, Pallas kernels, attend(): pl.pallas_call(attend_kernel, out_shape=(pltpu.VMEM(near.shape, F32), plt...  4.59 us
    pallas_call x2, Pallas kernels, load(): pl.pallas_call(functools.partial(load_kernel, starts=tuple((start for _,...  3.17 us
    ppermute x4, waiting for transfers between devices, swap(): return lax.ppermute(x, 'ctx', partners)  2.38 us
  transfers between devices with their start and end apart: 4, of which 2 were waited for; matrix products, arithmetic and copies ran while one was open for 0% of the time, Pallas kernels for 4%

profile of v2, /device:TPU:0, one launch (start us, length us, event | category | flops | bytes accessed | tf_op | source)
XLA Modules:
  0.0 83.3 jit_solution(10311994476565540484)
XLA Ops:
  0.0 0.0 copy-start
  0.0 0.9 %pack.1 = bf16[8,9,16,128]{3,2,1,0:T(8,128)(2,1)S(1)} custom-call(s32[2]{0:T(128)} %lengths_hbm.1, bf16[2,8192]{1,0:T(2,128)(2,1)} %q_hbm.1), custom_call_target="tpu_custom_call" | custom-call | tf_op jit(solution)/shard_map/pack/pallas_call | solution.py:66
  0.9 17.4 %all_to_all.20.near_ref = bf16[8,9,16,128]{3,2,1,0:T(8,128)(2,1)S(1)} all-to-all(bf16[8,9,16,128]{3,2,1,0:T(8,128)(2,1)S(1)} %pack.1), channel_id=1, replica_groups={{0,4,8,12,14,10,6,2},{1,5,9,13,15,11,7,3},{16,20,24,28,30,26,22,18},{17..., dimensions={0} | all-to-all | bytes 589824 | tf_op jit(solution)/shard_map/all_to_all | solution.py:355
  18.3 0.0 collective-permute-start
  18.3 1.6 %load.2 = (bf16[512,1024]{1,0:T(8,128)(2,1)S(1)}, bf16[512,1024]{1,0:T(8,128)(2,1)S(1)}, s32[1,512]{1,0:T(1,128)S(1)}) custom-call(bf16[512,1024]{1,0:T(8,128)(2,1)} %refs_0_, bf16[512,1024]{1,0:T(8,128)(2,1)} %refs_1_.1, s32[1,512]{1,0:T(1,128)} %bitcast.19), custom_call_target="tpu_custom_call" | custom-call | bytes 4196352 | tf_op jit(solution)/shard_map/load/pallas_call | solution.py:98
  19.9 0.0 collective-permute-done.far_ref
  19.9 4.6 %attend.1 = (f32[8,9,16,128]{3,2,1,0:T(8,128)S(1)}, bf16[8,9,16,128]{3,2,1,0:T(8,128)(2,1)S(1)}, bf16[768,8192]{1,0:T(8,128)(2,1)S(1)}) custom-call(bf16[8,9,16,128]{3,2,1,0:T(8,128)(2,1)S(1)} %all_to_all.20.near_ref, bf16[8,9,16,128]{3,2,1,0:T(8,128)(2,1)S(1)} %collective-permute-done.far_ref, s32[1,512]{1,0:T(1,128)S(1)} %get-tuple-element.19.position_ref, ...), custom_call_target="tpu_custom_call" | custom-call | flops 603979776 | bytes 2097152 | tf_op jit(solution)/shard_map/attend/pallas_call | solution.py:152
  24.5 0.6 collective-permute-start.1
  25.1 1.2 %collective-permute-done.1.came_ref = bf16[8,9,16,128]{3,2,1,0:T(8,128)(2,1)S(1)} collective-permute-done((bf16[8,9,16,128]{3,2,1,0:T(8,128)(2,1)S(1)}, bf16[8,9,16,128]{3,2,1,0:T(8,128)(2,1)S(1)}, u32[]{:S(2)}, u32[]{:S(2)}) %collective-permute-start.1) | collective-permute-done | bytes 294944 | tf_op jit(solution)/shard_map/ppermute | solution.py:358
  26.3 0.6 merge.1
  27.0 13.5 %all_to_all.21.parts_ref = bf16[8,9,16,128]{3,2,1,0:T(8,128)(2,1)S(1)} all-to-all(bf16[8,9,16,128]{3,2,1,0:T(8,128)(2,1)S(1)} %merge.1), channel_id=1, replica_groups={{0,4,8,12,14,10,6,2},{1,5,9,13,15,11,7,3},{16,20,24,28,30,26,22,18},{17..., dimensions={0} | all-to-all | bytes 589824 | tf_op jit(solution)/shard_map/all_to_all | solution.py:355
  40.5 0.0 copy-done
  40.5 0.5 finish.1
  41.0 11.6 %all_to_all.22 = bf16[8,2,8192]{2,1,0:T(2,128)(2,1)S(1)} all-to-all(bf16[8,2,8192]{2,1,0:T(2,128)(2,1)S(1)} %finish.1), channel_id=1, replica_groups={{0,4,8,12,14,10,6,2},{1,5,9,13,15,11,7,3},{16,20,24,28,30,26,22,18},{17..., dimensions={0} | all-to-all | bytes 524288 | tf_op jit(solution)/shard_map/all_to_all | solution.py:355
  52.6 0.2 slice_bitcast_fusion.7
  52.8 0.4 pad_maximum_fusion.near_ref
  53.2 0.1 collective-permute-start.2
  53.2 1.6 %load.3.gate_b_ref = bf16[128,8192]{1,0:T(8,128)(2,1)S(1)} custom-call(bf16[896,8192]{1,0:T(8,128)(2,1)} %refs_0_.1), custom_call_target="tpu_custom_call" | custom-call | bytes 29360128 | tf_op jit(solution)/shard_map/load/pallas_call | solution.py:98
  54.9 0.0 collective-permute-done.2.far_ref
  54.9 13.1 %feed_forward.1 = (f32[16,8192]{1,0:T(8,128)S(1)}, bf16[16,8192]{1,0:T(8,128)(2,1)S(1)}) custom-call(bf16[16,8192]{1,0:T(8,128)(2,1)S(1)} %pad_maximum_fusion.near_ref, bf16[16,8192]{1,0:T(8,128)(2,1)S(1)} %collective-permute-done.2.far_ref, bf16[768,8192]{1,0:T(8,128)(2,1)S(1)} %get-tuple-element.25.gate_a_ref, bf16[128,8192]{1,0:T(8,128)(2,1)S(1)} %load.3.gate_b_ref, ...), custom_call_target="tpu_custom_call" | custom-call | flops 1409286144 | bytes 29360128 | tf_op jit(solution)/shard_map/feed_forward/pallas_call | solution.py:306
  68.0 0.6 collective-permute-start.3
  68.6 1.2 %collective-permute-done.3 = bf16[16,8192]{1,0:T(8,128)(2,1)S(1)} collective-permute-done((bf16[16,8192]{1,0:T(8,128)(2,1)S(1)}, bf16[16,8192]{1,0:T(8,128)(2,1)S(1)}, u32[]{:S(2)}, u32[]{:S(2)}) %collective-permute-start.3) | collective-permute-done | bytes 262176 | tf_op jit(solution)/shard_map/ppermute | solution.py:358
  69.8 0.2 reshape.11
  70.0 12.5 %all_to_all.23 = bf16[8,2,8192]{2,1,0:T(2,128)(2,1)S(1)} all-to-all(bf16[8,2,8192]{2,1,0:T(2,128)(2,1)S(1)} %reshape.11), channel_id=1, replica_groups={{0,4,8,12,14,10,6,2},{1,5,9,13,15,11,7,3},{16,20,24,28,30,26,22,18},{17..., dimensions={0} | all-to-all | bytes 524288 | tf_op jit(solution)/shard_map/all_to_all | solution.py:355
  82.5 0.9 %reduce_sum.12 = bf16[2,8192]{1,0:T(2,128)(2,1)} reduce(bf16[8,2,8192]{2,1,0:T(2,128)(2,1)S(1)} %all_to_all.23, bf16[]{:T(256)} %constant.4.clone.1), dimensions={0}, to_apply=%region_0.0 | reduce | flops 114688 | bytes 294914 | tf_op jit(solution)/shard_map/reduce_sum | solution.py:376
  (1 shorter events, 0.0 us)
Async XLA Ops:
  0.0 40.5 %copy-start = (f32[8192]{0:T(1024)S(1)}, f32[8192]{0:T(1024)}, u32[]{:S(2)}) copy-start(f32[8192]{0:T(1024)} %param.14) | copy-start | bytes 98308
  18.3 1.6 %collective-permute-start = (bf16[8,9,16,128]{3,2,1,0:T(8,128)(2,1)S(1)}, bf16[8,9,16,128]{3,2,1,0:T(8,128)(2,1)S(1)}, u32[]{:S(2)}, u32[]{:S(2)}) collective-permute-start(bf16[8,9,16,128]{3,2,1,0:T(8,128)(2,1)S(1)} %all_to_all.20.near_ref), channel_id=1, source_target_pairs={{0,1},{1,0},{2,3},{3,2},{4,5},{5,4},{6,7},{7,6},{8,9},{9,8},{10,11... | collective-permute-start | bytes 884744 | tf_op jit(solution)/shard_map/ppermute | solution.py:358
  24.5 1.8 %collective-permute-start.1 = (bf16[8,9,16,128]{3,2,1,0:T(8,128)(2,1)S(1)}, bf16[8,9,16,128]{3,2,1,0:T(8,128)(2,1)S(1)}, u32[]{:S(2)}, u32[]{:S(2)}) collective-permute-start(bf16[8,9,16,128]{3,2,1,0:T(8,128)(2,1)S(1)} %get-tuple-element.24), channel_id=1, source_target_pairs={{0,1},{1,0},{2,3},{3,2},{4,5},{5,4},{6,7},{7,6},{8,9},{9,8},{10,11... | collective-permute-start | bytes 884744 | tf_op jit(solution)/shard_map/ppermute | solution.py:358
  53.2 1.7 %collective-permute-start.2 = (bf16[16,8192]{1,0:T(8,128)(2,1)S(1)}, bf16[16,8192]{1,0:T(8,128)(2,1)S(1)}, u32[]{:S(2)}, u32[]{:S(2)}) collective-permute-start(bf16[16,8192]{1,0:T(8,128)(2,1)S(1)} %pad_maximum_fusion.near_ref), channel_id=1, source_target_pairs={{0,1},{1,0},{2,3},{3,2},{4,5},{5,4},{6,7},{7,6},{8,9},{9,8},{10,11... | collective-permute-start | bytes 786440 | tf_op jit(solution)/shard_map/ppermute | solution.py:358
  68.0 1.7 %collective-permute-start.3 = (bf16[16,8192]{1,0:T(8,128)(2,1)S(1)}, bf16[16,8192]{1,0:T(8,128)(2,1)S(1)}, u32[]{:S(2)}, u32[]{:S(2)}) collective-permute-start(bf16[16,8192]{1,0:T(8,128)(2,1)S(1)} %get-tuple-element.28), channel_id=1, source_target_pairs={{0,1},{1,0},{2,3},{3,2},{4,5},{5,4},{6,7},{7,6},{8,9},{9,8},{10,11... | collective-permute-start | bytes 786440 | tf_op jit(solution)/shard_map/ppermute | solution.py:358

commit v3 on v2

v3 whole, which is shorter than its diff:
```python
import functools
import math

import jax
import jax.numpy as jnp
from jax import lax
from jax.experimental import pallas as pl
from jax.experimental.pallas import tpu as pltpu
from jax.sharding import PartitionSpec as P

D = 8192
QUERY_HEADS = 64
KEY_VALUE_HEADS = 8
HEAD_SIZE = 128
GROUP = QUERY_HEADS // KEY_VALUE_HEADS
F32 = jnp.float32
BF16 = jnp.bfloat16
SCALE = HEAD_SIZE ** (-0.5) * math.log2(math.e)
DEAD = -1e30
ROWS_BY_ROWS = (((1,), (1,)), ((), ()))
VMEM = pl.BlockSpec(memory_space=pltpu.VMEM)
ANY = pl.BlockSpec(memory_space=pl.ANY)
MIB = 1 << 20


def in_vmem(x):
    return pltpu.with_memory_space_constraint(x, pltpu.VMEM)


def in_hbm(x):
    return pltpu.with_memory_space_constraint(x, pltpu.HBM)


def rounded(x):
    return x.astype(BF16).astype(F32)


def pack_kernel(lengths_hbm, q_hbm, out_ref, slab_ref, lengths_ref, q_ref, sems):
    rows = q_ref.shape[0]
    copies = (
        pltpu.make_async_copy(q_hbm, q_ref, sems.at[0]),
        pltpu.make_async_copy(lengths_hbm, lengths_ref, sems.at[1]),
    )
    for copy in copies:
        copy.start()
    for copy in copies:
        copy.wait()
    q = q_ref[...].astype(F32)
    lane = lax.broadcasted_iota(jnp.int32, (GROUP, HEAD_SIZE), 1)
    for row in range(rows):
        for head in range(QUERY_HEADS):
            slot = row * GROUP + head % GROUP
            slab_ref[head // GROUP, slot : slot + 1, :] = q[
                row : row + 1, head * HEAD_SIZE : (head + 1) * HEAD_SIZE
            ]
        length = lengths_ref[row]
        high, low = (length >> 8).astype(F32), (length & 255).astype(F32)
        slab_ref[KEY_VALUE_HEADS, row * GROUP : (row + 1) * GROUP, :] = jnp.where(
            lane == 0, high, jnp.where(lane == 1, low, 0.0)
        )
    packed = slab_ref[...].astype(BF16)
    for peer in range(out_ref.shape[0]):
        out_ref[peer] = packed


def pack(queries, lengths, peers):
    slots = queries.shape[0] * GROUP
    shape = (KEY_VALUE_HEADS + 1, slots, HEAD_SIZE)
    return pl.pallas_call(
        pack_kernel,
        out_shape=pltpu.VMEM((peers,) + shape, BF16),
        in_specs=[ANY, ANY],
        out_specs=VMEM,
        scratch_shapes=[
            pltpu.VMEM(shape, F32),
            pltpu.SMEM(lengths.shape, lengths.dtype),
            pltpu.VMEM(queries.shape, queries.dtype),
            pltpu.SemaphoreType.DMA((2,)),
        ],
        compiler_params=pltpu.CompilerParams(vmem_limit_bytes=4 * MIB),
        name="pack",
    )(in_hbm(lengths), in_hbm(queries))


def load_kernel(*refs, starts):
    count = len(starts)
    copies = [
        pltpu.make_async_copy(
            refs[i].at[pl.ds(start, refs[count + i].shape[0])], refs[count + i], refs[-1].at[i]
        )
        for i, start in enumerate(starts)
    ]
    for copy in copies:
        copy.start()
    for copy in copies:
        copy.wait()


def load(*entries):
    shapes = [((rows,) + a.shape[1:], a.dtype) for a, _, rows in entries]
    return pl.pallas_call(
        functools.partial(load_kernel, starts=tuple(start for _, start, _ in entries)),
        out_shape=tuple(pltpu.VMEM(*shape) for shape in shapes),
        in_specs=[ANY] * len(entries),
        out_specs=(VMEM,) * len(entries),
        scratch_shapes=[pltpu.SemaphoreType.DMA((len(entries),))],
        compiler_params=pltpu.CompilerParams(vmem_limit_bytes=MIB),
        cost_estimate=pl.CostEstimate(
            flops=0, bytes_accessed=sum(2 * rows * a.shape[1] for a, _, rows in entries), transcendentals=0
        ),
        name="load",
    )(*(in_hbm(a) for a, _, _ in entries))


def attend_kernel(q_ref, position_ref, k_ref, v_ref, out_ref):
    peers, _, slots, _ = q_ref.shape
    flat = (peers * slots, HEAD_SIZE)
    numbers = q_ref[:, KEY_VALUE_HEADS].reshape(flat).astype(F32)
    lengths = numbers[:, 0:1] * 256.0 + numbers[:, 1:2]
    bias = jnp.where(position_ref[...].astype(F32) < lengths, 0.0, DEAD)
    lane = lax.broadcasted_iota(jnp.int32, flat, 1)
    state = jnp.zeros(flat, F32)
    for g in range(KEY_VALUE_HEADS):
        columns = slice(g * HEAD_SIZE, (g + 1) * HEAD_SIZE)
        scores = lax.dot_general(
            q_ref[:, g].reshape(flat), k_ref[:, columns], ROWS_BY_ROWS, preferred_element_type=F32
        )
        scores = scores * SCALE + bias
        peak = rounded(jnp.maximum(jnp.max(scores, axis=1, keepdims=True), 0.1 * DEAD))
        weights = jnp.exp2(scores - peak)
        total = jnp.sum(weights, axis=1, keepdims=True)
        summed = jnp.dot(weights.astype(BF16), v_ref[:, columns], preferred_element_type=F32)
        total_high = rounded(total)
        for index, column in enumerate((peak, total_high, total - total_high)):
            state = jnp.where(lane == index * KEY_VALUE_HEADS + g, column, state)
        out_ref[:, g] = summed.astype(out_ref.dtype).reshape(peers, slots, HEAD_SIZE)
    out_ref[:, KEY_VALUE_HEADS] = state.astype(out_ref.dtype).reshape(peers, slots, HEAD_SIZE)


def attend(q, position, keys, values, dtype):
    cells = q.size // HEAD_SIZE * keys.shape[0]
    return pl.pallas_call(
        attend_kernel,
        out_shape=pltpu.VMEM(q.shape, dtype),
        in_specs=[VMEM] * 4,
        out_specs=VMEM,
        compiler_params=pltpu.CompilerParams(vmem_limit_bytes=8 * MIB + 16 * q.size),
        cost_estimate=pl.CostEstimate(
            flops=4 * cells * HEAD_SIZE, bytes_accessed=4 * keys.size, transcendentals=cells
        ),
        name="attend",
    )(*(in_vmem(x) for x in (q, position, keys, values)))


def joined(states):
    lane = lax.broadcasted_iota(jnp.int32, states[0].shape, 1)
    peak = functools.reduce(jnp.maximum, states)
    scales = [jnp.exp2(state - peak) for state in states]
    total = jnp.zeros_like(peak)
    for state, scale in zip(states, scales):
        high = jnp.where(lane < 2 * KEY_VALUE_HEADS, state, 0.0)
        low = pltpu.roll(state, HEAD_SIZE - KEY_VALUE_HEADS, 1)
        total += (high + low) * pltpu.roll(scale, KEY_VALUE_HEADS, 1)
    return lane, peak, scales, total


def combine_kernel(*refs, count, order):
    sources, targets = refs[:count], refs[count:]
    per_target = targets[0].shape[0]
    chip = lax.axis_index("ctx") // 2 if order is not None else 0
    for place in range(per_target * len(targets)):
        index = place if order is None else chip ^ (order[place] // 2)
        target = targets[place // per_target].at[place % per_target]
        states = [ref[index, KEY_VALUE_HEADS].astype(F32) for ref in sources]
        lane, peak, scales, total = joined(states)
        high = rounded(total)
        low = pltpu.roll(total - high, KEY_VALUE_HEADS, 1)
        state = jnp.where(
            lane < KEY_VALUE_HEADS,
            peak,
            jnp.where(
                lane < 2 * KEY_VALUE_HEADS, high, jnp.where(lane < 3 * KEY_VALUE_HEADS, low, 0.0)
            ),
        )
        target[KEY_VALUE_HEADS] = state.astype(BF16)
        for g in range(KEY_VALUE_HEADS):
            target[g] = sum(
                ref[index, g].astype(F32) * scale[:, g : g + 1]
                for ref, scale in zip(sources, scales)
            ).astype(BF16)


def combine(sources, pieces, order=None):
    blocks = sources[0].shape[0] // pieces
    return pl.pallas_call(
        functools.partial(combine_kernel, count=len(sources), order=order),
        out_shape=(pltpu.VMEM((blocks,) + sources[0].shape[1:], BF16),) * pieces,
        in_specs=[VMEM] * len(sources),
        out_specs=(VMEM,) * pieces,
        compiler_params=pltpu.CompilerParams(vmem_limit_bytes=4 * MIB),
        name="combine",
    )(*(in_vmem(x) for x in sources))


def finish_kernel(mine_ref, came_ref, gain_ref, out_ref, row_ref):
    blocks, _, slots, _ = mine_ref.shape
    rows = slots // GROUP
    for block in range(blocks):
        pair = (mine_ref.at[block], came_ref.at[blocks - 1 - block])
        _, _, scales, total = joined([ref[KEY_VALUE_HEADS].astype(F32) for ref in pair])
        attended = []
        squares = jnp.zeros((slots, HEAD_SIZE), F32)
        for g in range(KEY_VALUE_HEADS):
            summed = sum(
                ref[g].astype(F32) * scale[:, g : g + 1] for ref, scale in zip(pair, scales)
            )
            one = rounded(summed / total[:, KEY_VALUE_HEADS + g : KEY_VALUE_HEADS + g + 1])
            squares += one * one
            attended.append(one)
        mean_square = (
            jnp.sum(squares.reshape(rows, GROUP, HEAD_SIZE), axis=(1, 2), keepdims=True) / D + 1e-05
        )
        inverse = lax.rsqrt(mean_square)
        for g in range(KEY_VALUE_HEADS):
            normed = attended[g].reshape(rows, GROUP, HEAD_SIZE) * inverse * gain_ref[g][None]
            for row in range(rows):
                place = block * rows + row
                for head in range(GROUP):
                    start = (g * GROUP + head) * HEAD_SIZE
                    row_ref[place : place + 1, start : start + HEAD_SIZE] = normed[
                        row, head : head + 1
                    ]
    out_ref[...] = row_ref[...].astype(BF16)


def finish(mine, came, norm_gain):
    rows = mine.shape[0] * mine.shape[2] // GROUP
    return pl.pallas_call(
        finish_kernel,
        out_shape=pltpu.VMEM((rows, D), BF16),
        in_specs=[VMEM] * 3,
        out_specs=VMEM,
        scratch_shapes=[pltpu.VMEM((rows, D), F32)],
        compiler_params=pltpu.CompilerParams(vmem_limit_bytes=4 * MIB),
        name="finish",
    )(in_vmem(mine), in_vmem(came), norm_gain.reshape(KEY_VALUE_HEADS, GROUP, HEAD_SIZE))


def feed_forward_kernel(
    near_ref, far_ref, gate_a_ref, gate_b_ref, up_a_ref, up_hbm, down_hbm, keep_ref, send_ref,
    x_ref, up_b_ref, down_ref, up_sem, down_sems,
):
    half, width = near_ref.shape
    downs = down_sems.shape[0]
    step = width // downs
    parts = [pl.ds(i * step, step) for i in range(downs)]
    up_rows = up_b_ref.shape[0]
    up_copy = pltpu.make_async_copy(
        up_hbm.at[pl.ds(up_hbm.shape[0] - up_rows, up_rows)], up_b_ref, up_sem
    )
    down_copies = [
        pltpu.make_async_copy(down_hbm.at[:, part], down_ref.at[:, part], down_sems.at[i])
        for i, part in enumerate(parts)
    ]

    up_copy.start()
    x_ref[:half] = near_ref[...]
    x_ref[half:] = far_ref[...]
    x = x_ref[...]

    def project(weight_ref):
        return lax.dot_general(x, weight_ref[...], ROWS_BY_ROWS, preferred_element_type=F32)

    gate = [project(gate_a_ref)]
    down_copies[0].start()
    gate.append(project(gate_b_ref))
    gate = jnp.concatenate(gate, axis=1)
    gate = gate / (1.0 + jnp.exp(-gate))
    down_copies[1].start()
    upward = [project(up_a_ref)]
    up_copy.wait()
    down_copies[2].start()
    upward.append(project(up_b_ref))
    activated = (gate * jnp.concatenate(upward, axis=1)).astype(BF16)
    for i, part in enumerate(parts):
        if i + 3 < downs:
            down_copies[i + 3].start()
        down_copies[i].wait()
        out = jnp.dot(activated, down_ref[:, part], preferred_element_type=F32)
        keep_ref[:, part] = out[:half]
        send_ref[:, part] = out[half:].astype(BF16)


def feed_forward(near, far, gate_a, gate_b, up_a, up, down):
    half, width = near.shape
    downs = 4
    return pl.pallas_call(
        feed_forward_kernel,
        out_shape=(pltpu.VMEM(near.shape, F32), pltpu.VMEM(near.shape, BF16)),
        in_specs=[VMEM] * 5 + [ANY, ANY],
        out_specs=(VMEM, VMEM),
        scratch_shapes=[
            pltpu.VMEM((2 * half, width), BF16),
            pltpu.VMEM((up.shape[0] - up_a.shape[0], width), up.dtype),
            pltpu.VMEM(down.shape, down.dtype),
            pltpu.SemaphoreType.DMA,
            pltpu.SemaphoreType.DMA((downs,)),
        ],
        compiler_params=pltpu.CompilerParams(vmem_limit_bytes=28 * MIB),
        cost_estimate=pl.CostEstimate(
            flops=12 * half * up.size, bytes_accessed=3 * down.size, transcendentals=half * up.shape[0]
        ),
        name="feed_forward",
    )(*(in_vmem(x) for x in (near, far, gate_a, gate_b, up_a)), in_hbm(up), in_hbm(down))


def spread_kernel(keep_ref, came_ref, out_ref, *, masks):
    chip = lax.axis_index("ctx") // 2
    rows = out_ref.shape[1]
    for k, mask in enumerate(masks):
        part = slice(k * rows, (k + 1) * rows)
        share = keep_ref[part] + came_ref[part].astype(F32)
        out_ref[chip ^ (mask // 2)] = share.astype(BF16)


def spread(keep, came, masks):
    rows = keep.shape[0] // len(masks)
    return pl.pallas_call(
        functools.partial(spread_kernel, masks=masks),
        out_shape=pltpu.VMEM((len(masks), rows, keep.shape[1]), BF16),
        in_specs=[VMEM, VMEM],
        out_specs=VMEM,
        compiler_params=pltpu.CompilerParams(vmem_limit_bytes=4 * MIB),
        name="spread",
    )(in_vmem(keep), in_vmem(came))


def stacked(blocks):
    total, offset, out = sum(b.shape[0] for b in blocks), 0, None
    for block in blocks:
        rows = block.shape[0]
        edges = ((offset, total - offset - rows, 0), (0, 0, 0))
        placed = lax.pad(block, jnp.array(-jnp.inf, block.dtype), edges)
        out = placed if out is None else jnp.maximum(out, placed)
        offset += rows
    return out


def rounds_of(devices):
    rounds, bit, width = [], 2, 1
    while bit < devices:
        width = min(width, (devices // bit).bit_length() - 1)
        rounds.append([m * bit for m in range((1 << width) - 1, 0, -1)])
        bit, width = bit << width, 2
    return rounds


def order_of(rounds):
    masks = [0]
    for moves in rounds:
        masks = [mask ^ move for move in [0] + moves for mask in masks]
    return tuple(masks)


def trade(arrays, moves, devices, entry=None):
    if entry is not None:
        late, arrays = lax.optimization_barrier((entry[0], arrays))
    came = [
        lax.ppermute(array, "ctx", [(i, i ^ move) for i in range(devices)])
        for array, move in zip(arrays, moves)
    ]
    if entry is None:
        return came, None
    (part,) = load((late,) + entry[1:])
    return lax.optimization_barrier((came, part))


def local(
    queries,
    cached_key_rows,
    cached_value_rows,
    cache_position,
    lengths,
    norm_gain,
    gate_weight,
    up_weight,
    down_weight,
):
    devices = lax.axis_size("ctx")
    peers = devices // 2
    rows = queries.shape[0]
    same_core = [[2 * i + core for i in range(peers)] for core in range(2)]
    partners = [(i, i ^ 1) for i in range(devices)]

    def exchange(x):
        return lax.all_to_all(x, "ctx", 0, 0, axis_index_groups=same_core, tiled=True)

    def swap(x):
        return lax.ppermute(x, "ctx", partners)

    rounds = rounds_of(devices)
    order = order_of(rounds)
    hidden = gate_weight.shape[0]
    first = hidden // 2
    slots = cached_key_rows.shape[0]
    windows = [(gate_weight, 0, first), (gate_weight, first, hidden - first), (up_weight, 0, first)]
    loads = []

    near = exchange(pack(queries, lengths, peers))
    late_keys, near = lax.optimization_barrier((cached_key_rows, near))
    far = swap(near)
    keys, values, position = load(
        (late_keys, 0, slots), (cached_value_rows, 0, slots), (cache_position.reshape(1, -1), 0, 1)
    )
    send = attend(far, position, keys, values, BF16)
    late_near, send = lax.optimization_barrier((near, send))
    came = swap(send)
    keep = attend(late_near, position, keys, values, F32)

    parts = (keep, came)
    chips_order = order
    for number, moves in reversed(list(enumerate(rounds))[1:]):
        mine, *out = combine(parts, len(moves) + 1, chips_order)
        chips_order = None
        got, loaded = trade(out, moves, devices, windows[0] if not loads else None)
        loads += [] if loaded is None else [loaded]
        parts = (mine, *got)
    (mine,) = combine(parts, 1, chips_order)
    (came,), loaded = trade([mine], rounds[0], devices, windows[1])
    loads.append(loaded)
    block = finish(mine, came, norm_gain)
    for number, moves in enumerate(rounds[1:]):
        got, loaded = trade([block] * len(moves), moves, devices, windows[2] if number == 0 else None)
        loads += [] if loaded is None else [loaded]
        block = stacked([block, *got])
    keep, send = feed_forward(block, swap(block), *loads, up_weight, down_weight)
    shares = exchange(spread(keep, swap(send), order))
    return jnp.sum(shares.astype(F32), axis=0).astype(BF16)


def solution(mesh):
    placed = (
        P(("groups", "ctx"), None),
        P(("groups", "ctx"), None),
        P(("groups", "ctx"), None),
        P(("groups", "ctx")),
        P(("groups", "ctx")),
        P(),
        P("ctx", None),
        P("ctx", None),
        P("ctx", None),
    )
    return jax.shard_map(
        local, mesh=mesh, in_specs=placed, out_specs=P(("groups", "ctx"), None), check_vma=False
    )
```

time: 83.8 us -> 77.9 us (0.930)
  blocking collectives: 55.1 us -> 30.1 us
  starting transfers between devices: 1.2 us -> 10.5 us
  Pallas kernels: 22.9 us -> 30.3 us
  waiting for transfers between devices: 2.38 us -> 5.48 us
    all_to_all x4 -> x2, blocking collectives: 55.1 us -> 30.1 us  [exchange(): lax.all_to_all(x, 'ctx', 0, 0, axis_index_groups=same_core, tiled=True)]
    ppermute x0 -> x7, starting transfers between devices: none -> 9.64 us  [trade(): lax.ppermute(array, 'ctx', [(i, i ^ move) for i in range(devices)])]
    pallas_call x2 -> x4, Pallas kernels: 3.17 us -> 10.8 us  [load(): pl.pallas_call(functools.partial(load_kernel, starts=tuple((start for _,...]
    ppermute x0 -> x7, waiting for transfers between devices: none -> 2.54 us  [trade(): lax.ppermute(array, 'ctx', [(i, i ^ move) for i in range(devices)])]
    pallas_call x1, Pallas kernels: 13.1 us -> 11.8 us  [feed_forward(): pl.pallas_call(feed_forward_kernel, out_shape=(pltpu.VMEM(near.shape, F32...]
    pallas_call x3 -> x6, Pallas kernels: 5.72 us -> 6.74 us  [the longest x2 4.65 us: attend(): pl.pallas_call(attend_kernel, out_shape=pltpu.VMEM(q.shape, dtype), in_sp...]
  transfers between devices with their start and end apart: 4 -> 11, of which waited for: 2 -> 5; matrix products, arithmetic and copies ran while one was open for 0% -> 0% of each run, Pallas kernels for 4% -> 17%
where the time goes in v3:
time: 77.9 us; the launch traced here: 77.5 us
  Pallas kernels  30.3 us (39%)
  blocking collectives  30.1 us (39%)
  starting transfers between devices  10.5 us (13%)
  waiting for transfers between devices  5.48 us (7%)
  other arithmetic  1.01 us (1%)
    all_to_all x2, blocking collectives, exchange(): lax.all_to_all(x, 'ctx', 0, 0, axis_index_groups=same_core, tiled=True)  30.1 us
    pallas_call x1, Pallas kernels, feed_forward(): pl.pallas_call(feed_forward_kernel, out_shape=(pltpu.VMEM(near.shape, F32...  11.8 us
    pallas_call x4, Pallas kernels, load(): pl.pallas_call(functools.partial(load_kernel, starts=tuple((start for _,...  10.8 us
    ppermute x7, starting transfers between devices, trade(): lax.ppermute(array, 'ctx', [(i, i ^ move) for i in range(devices)])  9.64 us
    pallas_call x2, Pallas kernels, attend(): pl.pallas_call(attend_kernel, out_shape=pltpu.VMEM(q.shape, dtype), in_sp...  4.65 us
    ppermute x4, waiting for transfers between devices, swap(): return lax.ppermute(x, 'ctx', partners)  2.93 us
    ppermute x7, waiting for transfers between devices, trade(): lax.ppermute(array, 'ctx', [(i, i ^ move) for i in range(devices)])  2.54 us
  transfers between devices with their start and end apart: 11, of which 5 were waited for; matrix products, arithmetic and copies ran while one was open for 0% of the time, Pallas kernels for 17%

profile of v3, /device:TPU:0, one launch (start us, length us, event | category | flops | bytes accessed | tf_op | source)
XLA Modules:
  0.0 77.5 jit_solution(1243050807061620156)
XLA Ops:
  0.0 0.9 %pack.1 = bf16[8,9,16,128]{3,2,1,0:T(8,128)(2,1)S(1)} custom-call(s32[2]{0:T(128)} %lengths_hbm.1, bf16[2,8192]{1,0:T(2,128)(2,1)} %q_hbm.1), custom_call_target="tpu_custom_call" | custom-call | tf_op jit(solution)/shard_map/pack/pallas_call | solution.py:69
  0.9 17.4 %all_to_all.10.q_ref = bf16[8,9,16,128]{3,2,1,0:T(8,128)(2,1)S(1)} all-to-all(bf16[8,9,16,128]{3,2,1,0:T(8,128)(2,1)S(1)} %pack.1), channel_id=1, replica_groups={{0,2,4,6,8,10,12,14},{1,3,5,7,9,11,13,15},{16,18,20,22,24,26,28,30},{17..., dimensions={0} | all-to-all | bytes 589824 | tf_op jit(solution)/shard_map/all_to_all | solution.py:396
  18.3 1.6 %load.4 = (bf16[512,1024]{1,0:T(8,128)(2,1)S(1)}, bf16[512,1024]{1,0:T(8,128)(2,1)S(1)}, s32[1,512]{1,0:T(1,128)S(1)}) custom-call(bf16[512,1024]{1,0:T(8,128)(2,1)} %refs_0_, bf16[512,1024]{1,0:T(8,128)(2,1)} %refs_1_.1, s32[1,512]{1,0:T(1,128)} %bitcast.3), custom_call_target="tpu_custom_call" | custom-call | bytes 2098176 | tf_op jit(solution)/shard_map/load/pallas_call | solution.py:101
  19.9 0.0 collective-permute-done.q_ref
  19.9 2.3 %attend.2 = bf16[8,9,16,128]{3,2,1,0:T(8,128)(2,1)S(1)} custom-call(bf16[8,9,16,128]{3,2,1,0:T(8,128)(2,1)S(1)} %collective-permute-done.q_ref, s32[1,512]{1,0:T(1,128)S(1)} %get-tuple-element.40.position_ref, bf16[512,1024]{1,0:T(8,128)(2,1)S(1)} %get-tuple-element.41.k_ref, bf16[512,1024]{1,0:T(8,128)(2,1)S(1)} %get-tuple-element.42.v_ref), custom_call_target="tpu_custom_call" | custom-call | flops 301989888 | bytes 2097152 | tf_op jit(solution)/shard_map/attend/pallas_call | solution.py:142
  22.2 0.6 collective-permute-start.1
  22.8 2.3 %attend.3.refs_0_ = f32[8,9,16,128]{3,2,1,0:T(8,128)S(1)} custom-call(bf16[8,9,16,128]{3,2,1,0:T(8,128)(2,1)S(1)} %all_to_all.10.q_ref, s32[1,512]{1,0:T(1,128)S(1)} %get-tuple-element.40.position_ref, bf16[512,1024]{1,0:T(8,128)(2,1)S(1)} %get-tuple-element.41.k_ref, bf16[512,1024]{1,0:T(8,128)(2,1)S(1)} %get-tuple-element.42.v_ref), custom_call_target="tpu_custom_call" | custom-call | flops 301989888 | bytes 2097152 | tf_op jit(solution)/shard_map/attend/pallas_call | solution.py:142
  25.2 1.0 %combine.2 = (bf16[2,9,16,128]{3,2,1,0:T(8,128)(2,1)S(1)}, bf16[2,9,16,128]{3,2,1,0:T(8,128)(2,1)S(1)}, bf16[2,9,16,128]{3,2,1,0:T(8,128)(2,1)S(1)}, bf16[2,9,16,128]{3,2,1,0:T(8,128)(2,1)S(1)}) custom-call(f32[8,9,16,128]{3,2,1,0:T(8,128)S(1)} %attend.3.refs_0_, bf16[8,9,16,128]{3,2,1,0:T(8,128)(2,1)S(1)} %collective-permute-done.1.refs_1_), custom_call_target="tpu_custom_call" | custom-call | tf_op jit(solution)/shard_map/combine/pallas_call | solution.py:195
  26.2 1.5 %collective-permute-start.2 = (bf16[2,9,16,128]{3,2,1,0:T(8,128)(2,1)S(1)}, bf16[2,9,16,128]{3,2,1,0:T(8,128)(2,1)S(1)}, u32[]{:S(2)}, u32[]{:S(2)}) collective-permute-start(bf16[2,9,16,128]{3,2,1,0:T(8,128)(2,1)S(1)} %get-tuple-element.49), channel_id=1, source_target_pairs={{0,12},{1,13},{2,14},{3,15},{4,8},{5,9},{6,10},{7,11},{8,4},{9,5},... | collective-permute-start | bytes 221192 | tf_op jit(solution)/shard_map/ppermute | solution.py:369
  27.7 0.6 collective-permute-start.3
  28.3 2.3 %collective-permute-start.4 = (bf16[2,9,16,128]{3,2,1,0:T(8,128)(2,1)S(1)}, bf16[2,9,16,128]{3,2,1,0:T(8,128)(2,1)S(1)}, u32[]{:S(2)}, u32[]{:S(2)}) collective-permute-start(bf16[2,9,16,128]{3,2,1,0:T(8,128)(2,1)S(1)} %get-tuple-element.51), channel_id=1, source_target_pairs={{0,4},{1,5},{2,6},{3,7},{4,0},{5,1},{6,2},{7,3},{8,12},{9,13},{10,... | collective-permute-start | bytes 221192 | tf_op jit(solution)/shard_map/ppermute | solution.py:369
  30.6 3.1 %load.5.gate_a_ref = bf16[448,8192]{1,0:T(8,128)(2,1)S(1)} custom-call(bf16[896,8192]{1,0:T(8,128)(2,1)} %refs_0_.2), custom_call_target="tpu_custom_call" | custom-call | bytes 7340032 | tf_op jit(solution)/shard_map/load/pallas_call | solution.py:101
  33.7 0.0 copy-start
  33.7 1.7 %collective-permute-done.3.refs_2_ = bf16[2,9,16,128]{3,2,1,0:T(8,128)(2,1)S(1)} collective-permute-done((bf16[2,9,16,128]{3,2,1,0:T(8,128)(2,1)S(1)}, bf16[2,9,16,128]{3,2,1,0:T(8,128)(2,1)S(1)}, u32[]{:S(2)}, u32[]{:S(2)}) %collective-permute-start.3) | collective-permute-done | bytes 73760 | tf_op jit(solution)/shard_map/ppermute | solution.py:369
  35.4 0.3 combine.3.mine_ref
  35.7 0.7 collective-permute-start.5
  36.5 3.1 %load.6.gate_b_ref = bf16[448,8192]{1,0:T(8,128)(2,1)S(1)} custom-call(bf16[896,8192]{1,0:T(8,128)(2,1)} %refs_0_.2), custom_call_target="tpu_custom_call" | custom-call | bytes 7340032 | tf_op jit(solution)/shard_map/load/pallas_call | solution.py:101
  39.6 0.6 collective-permute-done.5.came_ref
  40.2 0.5 finish.1
  40.7 1.5 %collective-permute-start.6 = (bf16[4,8192]{1,0:T(4,128)(2,1)S(1)}, bf16[4,8192]{1,0:T(4,128)(2,1)S(1)}, u32[]{:S(2)}, u32[]{:S(2)}) collective-permute-start(bf16[4,8192]{1,0:T(4,128)(2,1)S(1)} %finish.1), channel_id=1, source_target_pairs={{0,12},{1,13},{2,14},{3,15},{4,8},{5,9},{6,10},{7,11},{8,4},{9,5},... | collective-permute-start | bytes 196616 | tf_op jit(solution)/shard_map/ppermute | solution.py:369
  42.2 2.9 %collective-permute-start.8 = (bf16[4,8192]{1,0:T(4,128)(2,1)S(1)}, bf16[4,8192]{1,0:T(4,128)(2,1)S(1)}, u32[]{:S(2)}, u32[]{:S(2)}) collective-permute-start(bf16[4,8192]{1,0:T(4,128)(2,1)S(1)} %finish.1), channel_id=1, source_target_pairs={{0,4},{1,5},{2,6},{3,7},{4,0},{5,1},{6,2},{7,3},{8,12},{9,13},{10,... | collective-permute-start | bytes 196616 | tf_op jit(solution)/shard_map/ppermute | solution.py:369
  45.1 3.1 %load.7.up_a_ref = bf16[448,8192]{1,0:T(8,128)(2,1)S(1)} custom-call(bf16[896,8192]{1,0:T(8,128)(2,1)} %up_hbm.1), custom_call_target="tpu_custom_call" | custom-call | bytes 7340032 | tf_op jit(solution)/shard_map/load/pallas_call | solution.py:101
  48.3 0.3 collective-permute-done.7
  48.5 0.2 pad_maximum_fusion.near_ref
  48.7 0.1 collective-permute-start.9
  48.8 1.5 %collective-permute-done.9.far_ref = bf16[16,8192]{1,0:T(8,128)(2,1)S(1)} collective-permute-done((bf16[16,8192]{1,0:T(8,128)(2,1)S(1)}, bf16[16,8192]{1,0:T(8,128)(2,1)S(1)}, u32[]{:S(2)}, u32[]{:S(2)}) %collective-permute-start.9) | collective-permute-done | bytes 262176 | tf_op jit(solution)/shard_map/ppermute | solution.py:399
  50.3 11.8 %feed_forward.1 = (f32[16,8192]{1,0:T(8,128)S(1)}, bf16[16,8192]{1,0:T(8,128)(2,1)S(1)}) custom-call(bf16[16,8192]{1,0:T(8,128)(2,1)S(1)} %pad_maximum_fusion.near_ref, bf16[16,8192]{1,0:T(8,128)(2,1)S(1)} %collective-permute-done.9.far_ref, bf16[448,8192]{1,0:T(8,128)(2,1)S(1)} %load.5.gate_a_ref, bf16[448,8192]{1,0:T(8,128)(2,1)S(1)} %load.6.gate_b_ref, ...), custom_call_target="tpu_custom_call" | custom-call | flops 1409286144 | bytes 22020096 | tf_op jit(solution)/shard_map/feed_forward/pallas_call | solution.py:297
  62.1 0.2 collective-permute-start.10
  62.3 1.4 %collective-permute-done.10.came_ref = bf16[16,8192]{1,0:T(8,128)(2,1)S(1)} collective-permute-done((bf16[16,8192]{1,0:T(8,128)(2,1)S(1)}, bf16[16,8192]{1,0:T(8,128)(2,1)S(1)}, u32[]{:S(2)}, u32[]{:S(2)}) %collective-permute-start.10) | collective-permute-done | bytes 262176 | tf_op jit(solution)/shard_map/ppermute | solution.py:399
  63.7 0.3 spread.1
  64.0 12.7 %all_to_all.11 = bf16[8,2,8192]{2,1,0:T(2,128)(2,1)S(1)} all-to-all(bf16[8,2,8192]{2,1,0:T(2,128)(2,1)S(1)} %spread.1), channel_id=1, replica_groups={{0,2,4,6,8,10,12,14},{1,3,5,7,9,11,13,15},{16,18,20,22,24,26,28,30},{17..., dimensions={0} | all-to-all | bytes 524288 | tf_op jit(solution)/shard_map/all_to_all | solution.py:396
  76.7 0.9 %reduce_sum.12 = bf16[2,8192]{1,0:T(2,128)(2,1)} reduce(bf16[8,2,8192]{2,1,0:T(2,128)(2,1)S(1)} %all_to_all.11, bf16[]{:T(256)} %constant.4.clone.1), dimensions={0}, to_apply=%region_0.0 | reduce | flops 114688 | bytes 294914 | tf_op jit(solution)/shard_map/reduce_sum | solution.py:438
  (8 shorter events, 0.0 us)
Async XLA Ops:
  18.3 1.6 %collective-permute-start = (bf16[8,9,16,128]{3,2,1,0:T(8,128)(2,1)S(1)}, bf16[8,9,16,128]{3,2,1,0:T(8,128)(2,1)S(1)}, u32[]{:S(2)}, u32[]{:S(2)}) collective-permute-start(bf16[8,9,16,128]{3,2,1,0:T(8,128)(2,1)S(1)} %all_to_all.10.q_ref), channel_id=1, source_target_pairs={{0,1},{1,0},{2,3},{3,2},{4,5},{5,4},{6,7},{7,6},{8,9},{9,8},{10,11... | collective-permute-start | bytes 884744 | tf_op jit(solution)/shard_map/ppermute | solution.py:399
  22.2 2.9 %collective-permute-start.1 = (bf16[8,9,16,128]{3,2,1,0:T(8,128)(2,1)S(1)}, bf16[8,9,16,128]{3,2,1,0:T(8,128)(2,1)S(1)}, u32[]{:S(2)}, u32[]{:S(2)}) collective-permute-start(bf16[8,9,16,128]{3,2,1,0:T(8,128)(2,1)S(1)} %attend.2), channel_id=1, source_target_pairs={{0,1},{1,0},{2,3},{3,2},{4,5},{5,4},{6,7},{7,6},{8,9},{9,8},{10,11... | collective-permute-start | bytes 884744 | tf_op jit(solution)/shard_map/ppermute | solution.py:399
  26.2 7.6 %collective-permute-start.2 = (bf16[2,9,16,128]{3,2,1,0:T(8,128)(2,1)S(1)}, bf16[2,9,16,128]{3,2,1,0:T(8,128)(2,1)S(1)}, u32[]{:S(2)}, u32[]{:S(2)}) collective-permute-start(bf16[2,9,16,128]{3,2,1,0:T(8,128)(2,1)S(1)} %get-tuple-element.49), channel_id=1, source_target_pairs={{0,12},{1,13},{2,14},{3,15},{4,8},{5,9},{6,10},{7,11},{8,4},{9,5},... | collective-permute-start | bytes 221192 | tf_op jit(solution)/shard_map/ppermute | solution.py:369
  27.7 7.7 %collective-permute-start.3 = (bf16[2,9,16,128]{3,2,1,0:T(8,128)(2,1)S(1)}, bf16[2,9,16,128]{3,2,1,0:T(8,128)(2,1)S(1)}, u32[]{:S(2)}, u32[]{:S(2)}) collective-permute-start(bf16[2,9,16,128]{3,2,1,0:T(8,128)(2,1)S(1)} %get-tuple-element.50), channel_id=1, source_target_pairs={{0,8},{1,9},{2,10},{3,11},{4,12},{5,13},{6,14},{7,15},{8,0},{9,1},... | collective-permute-start | bytes 221192 | tf_op jit(solution)/shard_map/ppermute | solution.py:369
  28.3 7.1 %collective-permute-start.4 = (bf16[2,9,16,128]{3,2,1,0:T(8,128)(2,1)S(1)}, bf16[2,9,16,128]{3,2,1,0:T(8,128)(2,1)S(1)}, u32[]{:S(2)}, u32[]{:S(2)}) collective-permute-start(bf16[2,9,16,128]{3,2,1,0:T(8,128)(2,1)S(1)} %get-tuple-element.51), channel_id=1, source_target_pairs={{0,4},{1,5},{2,6},{3,7},{4,0},{5,1},{6,2},{7,3},{8,12},{9,13},{10,... | collective-permute-start | bytes 221192 | tf_op jit(solution)/shard_map/ppermute | solution.py:369
  33.7 6.5 %copy-start = (f32[8192]{0:T(1024)S(1)}, f32[8192]{0:T(1024)}, u32[]{:S(2)}) copy-start(f32[8192]{0:T(1024)} %param.14) | copy-start | bytes 98308
  35.7 4.4 %collective-permute-start.5 = (bf16[2,9,16,128]{3,2,1,0:T(8,128)(2,1)S(1)}, bf16[2,9,16,128]{3,2,1,0:T(8,128)(2,1)S(1)}, u32[]{:S(2)}, u32[]{:S(2)}) collective-permute-start(bf16[2,9,16,128]{3,2,1,0:T(8,128)(2,1)S(1)} %combine.3.mine_ref), channel_id=1, source_target_pairs={{0,2},{1,3},{2,0},{3,1},{4,6},{5,7},{6,4},{7,5},{8,10},{9,11},{10,... | collective-permute-start | bytes 221192 | tf_op jit(solution)/shard_map/ppermute | solution.py:369
  40.7 7.6 %collective-permute-start.6 = (bf16[4,8192]{1,0:T(4,128)(2,1)S(1)}, bf16[4,8192]{1,0:T(4,128)(2,1)S(1)}, u32[]{:S(2)}, u32[]{:S(2)}) collective-permute-start(bf16[4,8192]{1,0:T(4,128)(2,1)S(1)} %finish.1), channel_id=1, source_target_pairs={{0,12},{1,13},{2,14},{3,15},{4,8},{5,9},{6,10},{7,11},{8,4},{9,5},... | collective-permute-start | bytes 196616 | tf_op jit(solution)/shard_map/ppermute | solution.py:369
  42.2 6.3 %collective-permute-start.7 = (bf16[4,8192]{1,0:T(4,128)(2,1)S(1)}, bf16[4,8192]{1,0:T(4,128)(2,1)S(1)}, u32[]{:S(2)}, u32[]{:S(2)}) collective-permute-start(bf16[4,8192]{1,0:T(4,128)(2,1)S(1)} %finish.1), channel_id=1, source_target_pairs={{0,8},{1,9},{2,10},{3,11},{4,12},{5,13},{6,14},{7,15},{8,0},{9,1},... | collective-permute-start | bytes 196616 | tf_op jit(solution)/shard_map/ppermute | solution.py:369
  42.2 6.3 %collective-permute-start.8 = (bf16[4,8192]{1,0:T(4,128)(2,1)S(1)}, bf16[4,8192]{1,0:T(4,128)(2,1)S(1)}, u32[]{:S(2)}, u32[]{:S(2)}) collective-permute-start(bf16[4,8192]{1,0:T(4,128)(2,1)S(1)} %finish.1), channel_id=1, source_target_pairs={{0,4},{1,5},{2,6},{3,7},{4,0},{5,1},{6,2},{7,3},{8,12},{9,13},{10,... | collective-permute-start | bytes 196616 | tf_op jit(solution)/shard_map/ppermute | solution.py:369
  48.7 1.6 %collective-permute-start.9 = (bf16[16,8192]{1,0:T(8,128)(2,1)S(1)}, bf16[16,8192]{1,0:T(8,128)(2,1)S(1)}, u32[]{:S(2)}, u32[]{:S(2)}) collective-permute-start(bf16[16,8192]{1,0:T(8,128)(2,1)S(1)} %pad_maximum_fusion.near_ref), channel_id=1, source_target_pairs={{0,1},{1,0},{2,3},{3,2},{4,5},{5,4},{6,7},{7,6},{8,9},{9,8},{10,11... | collective-permute-start | bytes 786440 | tf_op jit(solution)/shard_map/ppermute | solution.py:399
  62.1 1.6 %collective-permute-start.10 = (bf16[16,8192]{1,0:T(8,128)(2,1)S(1)}, bf16[16,8192]{1,0:T(8,128)(2,1)S(1)}, u32[]{:S(2)}, u32[]{:S(2)}) collective-permute-start(bf16[16,8192]{1,0:T(8,128)(2,1)S(1)} %get-tuple-element.70), channel_id=1, source_target_pairs={{0,1},{1,0},{2,3},{3,2},{4,5},{5,4},{6,7},{7,6},{8,9},{9,8},{10,11... | collective-permute-start | bytes 786440 | tf_op jit(solution)/shard_map/ppermute | solution.py:399

commit v4 on v3

--- a/solution.py
+++ b/solution.py
@@ -120,20 +120,35 @@
     bias = jnp.where(position_ref[...].astype(F32) < lengths, 0.0, DEAD)
     lane = lax.broadcasted_iota(jnp.int32, flat, 1)
     state = jnp.zeros(flat, F32)
+
+    def columns(g):
+        return slice(g * HEAD_SIZE, (g + 1) * HEAD_SIZE)
+
+    def score(g):
+        return lax.dot_general(
+            q_ref[:, g].reshape(flat), k_ref[:, columns(g)], ROWS_BY_ROWS, preferred_element_type=F32
+        )
+
+    def add_up(g, weights):
+        summed = jnp.dot(weights, v_ref[:, columns(g)], preferred_element_type=F32)
+        out_ref[:, g] = summed.astype(out_ref.dtype).reshape(peers, slots, HEAD_SIZE)
+
+    coming = score(0)
+    waiting = None
     for g in range(KEY_VALUE_HEADS):
-        columns = slice(g * HEAD_SIZE, (g + 1) * HEAD_SIZE)
-        scores = lax.dot_general(
-            q_ref[:, g].reshape(flat), k_ref[:, columns], ROWS_BY_ROWS, preferred_element_type=F32
-        )
-        scores = scores * SCALE + bias
+        scores = coming * SCALE + bias
+        if g + 1 < KEY_VALUE_HEADS:
+            coming = score(g + 1)
         peak = rounded(jnp.maximum(jnp.max(scores, axis=1, keepdims=True), 0.1 * DEAD))
         weights = jnp.exp2(scores - peak)
         total = jnp.sum(weights, axis=1, keepdims=True)
-        summed = jnp.dot(weights.astype(BF16), v_ref[:, columns], preferred_element_type=F32)
+        if waiting is not None:
+            add_up(g - 1, waiting)
+        waiting = weights.astype(BF16)
         total_high = rounded(total)
         for index, column in enumerate((peak, total_high, total - total_high)):
             state = jnp.where(lane == index * KEY_VALUE_HEADS + g, column, state)
-        out_ref[:, g] = summed.astype(out_ref.dtype).reshape(peers, slots, HEAD_SIZE)
+    add_up(KEY_VALUE_HEADS - 1, waiting)
     out_ref[:, KEY_VALUE_HEADS] = state.astype(out_ref.dtype).reshape(peers, slots, HEAD_SIZE)
 
 
@@ -166,26 +181,30 @@
 
 def combine_kernel(*refs, count, order):
     sources, targets = refs[:count], refs[count:]
-    per_target = targets[0].shape[0]
+    per_target, _, slots, _ = targets[0].shape
+    places = range(per_target * len(targets))
     chip = lax.axis_index("ctx") // 2 if order is not None else 0
-    for place in range(per_target * len(targets)):
-        index = place if order is None else chip ^ (order[place] // 2)
+    indices = [place if order is None else chip ^ (order[place] // 2) for place in places]
+    lane, peak, scales, total = joined(
+        [
+            jnp.concatenate([ref[index, KEY_VALUE_HEADS].astype(F32) for index in indices], axis=0)
+            for ref in sources
+        ]
+    )
+    high = rounded(total)
+    low = pltpu.roll(total - high, KEY_VALUE_HEADS, 1)
+    state = jnp.where(
+        lane < KEY_VALUE_HEADS,
+        peak,
+        jnp.where(lane < 2 * KEY_VALUE_HEADS, high, jnp.where(lane < 3 * KEY_VALUE_HEADS, low, 0.0)),
+    ).astype(BF16)
+    for place, index in zip(places, indices):
         target = targets[place // per_target].at[place % per_target]
-        states = [ref[index, KEY_VALUE_HEADS].astype(F32) for ref in sources]
-        lane, peak, scales, total = joined(states)
-        high = rounded(total)
-        low = pltpu.roll(total - high, KEY_VALUE_HEADS, 1)
-        state = jnp.where(
-            lane < KEY_VALUE_HEADS,
-            peak,
-            jnp.where(
-                lane < 2 * KEY_VALUE_HEADS, high, jnp.where(lane < 3 * KEY_VALUE_HEADS, low, 0.0)
-            ),
-        )
-        target[KEY_VALUE_HEADS] = state.astype(BF16)
+        part = slice(place * slots, (place + 1) * slots)
+        target[KEY_VALUE_HEADS] = state[part]
         for g in range(KEY_VALUE_HEADS):
             target[g] = sum(
-                ref[index, g].astype(F32) * scale[:, g : g + 1]
+                ref[index, g].astype(F32) * scale[part, g : g + 1]
                 for ref, scale in zip(sources, scales)
             ).astype(BF16)
 
@@ -314,25 +333,25 @@
     )(*(in_vmem(x) for x in (near, far, gate_a, gate_b, up_a)), in_hbm(up), in_hbm(down))
 
 
-def spread_kernel(keep_ref, came_ref, out_ref, *, masks):
-    chip = lax.axis_index("ctx") // 2
-    rows = out_ref.shape[1]
-    for k, mask in enumerate(masks):
-        part = slice(k * rows, (k + 1) * rows)
-        share = keep_ref[part] + came_ref[part].astype(F32)
-        out_ref[chip ^ (mask // 2)] = share.astype(BF16)
-
-
-def spread(keep, came, masks):
-    rows = keep.shape[0] // len(masks)
-    return pl.pallas_call(
-        functools.partial(spread_kernel, masks=masks),
-        out_shape=pltpu.VMEM((len(masks), rows, keep.shape[1]), BF16),
-        in_specs=[VMEM, VMEM],
-        out_specs=VMEM,
-        compiler_params=pltpu.CompilerParams(vmem_limit_bytes=4 * MIB),
-        name="spread",
-    )(in_vmem(keep), in_vmem(came))
+def share_kernel(*refs, count):
+    sources, targets = refs[:count], refs[count:]
+    rows = targets[0].shape[0]
+    total = sum(ref[...].astype(F32) for ref in sources)
+    for i, target in enumerate(targets):
+        target[...] = total[i * rows : (i + 1) * rows].astype(target.dtype)
+
+
+def share(sources, pieces):
+    rows, width = sources[0].shape
+    shape = (rows // pieces, width)
+    return pl.pallas_call(
+        functools.partial(share_kernel, count=len(sources)),
+        out_shape=(pltpu.VMEM(shape, F32),) + (pltpu.VMEM(shape, BF16),) * (pieces - 1),
+        in_specs=[VMEM] * len(sources),
+        out_specs=(VMEM,) * pieces,
+        compiler_params=pltpu.CompilerParams(vmem_limit_bytes=8 * MIB),
+        name="share",
+    )(*(in_vmem(x) for x in sources))
 
 
 def stacked(blocks):
@@ -350,7 +369,7 @@
     rounds, bit, width = [], 2, 1
     while bit < devices:
         width = min(width, (devices // bit).bit_length() - 1)
-        rounds.append([m * bit for m in range((1 << width) - 1, 0, -1)])
+        rounds.append([m * bit for m in ([2, 1, 3] if width == 2 else [1])])
         bit, width = bit << width, 2
     return rounds
 
@@ -434,8 +453,11 @@
         loads += [] if loaded is None else [loaded]
         block = stacked([block, *got])
     keep, send = feed_forward(block, swap(block), *loads, up_weight, down_weight)
-    shares = exchange(spread(keep, swap(send), order))
-    return jnp.sum(shares.astype(F32), axis=0).astype(BF16)
+    parts = (keep, swap(send))
+    for moves in reversed(rounds):
+        mine, *out = share(parts, len(moves) + 1)
+        parts = (mine, *trade(out, moves, devices)[0])
+    return sum(part.astype(F32) for part in parts).astype(BF16)
 
 
 def solution(mesh):

time: 77.9 us -> 75.2 us (0.965)
  blocking collectives: 30.1 us -> 17.4 us
  waiting for transfers between devices: 5.48 us -> 13.3 us
  starting transfers between devices: 10.5 us -> 15.7 us
  Pallas kernels: 30.3 us -> 27.4 us
    all_to_all x2 -> x1, blocking collectives: 30.1 us -> 17.4 us  [exchange(): lax.all_to_all(x, 'ctx', 0, 0, axis_index_groups=same_core, tiled=True)]
    ppermute x7 -> x11, waiting for transfers between devices: 2.54 us -> 10.4 us  [trade(): lax.ppermute(array, 'ctx', [(i, i ^ move) for i in range(devices)])]
    ppermute x7 -> x11, starting transfers between devices: 9.64 us -> 14.9 us  [trade(): lax.ppermute(array, 'ctx', [(i, i ^ move) for i in range(devices)])]
    pallas_call x2, Pallas kernels: 4.65 us -> 2.41 us  [attend(): pl.pallas_call(attend_kernel, out_shape=pltpu.VMEM(q.shape, dtype), in_sp...]
    reduce_sum x1 -> x0, other arithmetic: 0.85 us -> none  [local(): return jnp.sum(shares.astype(F32), axis=0).astype(BF16)]
  transfers between devices with their start and end apart: 11 -> 15, of which waited for: 5 -> 9; matrix products, arithmetic and copies ran while one was open for 0% -> 0% of each run, Pallas kernels for 17% -> 16%
where the time goes in v4:
time: 75.2 us; the launch traced here: 74.8 us
  Pallas kernels  27.4 us (36%)
  blocking collectives  17.4 us (23%)
  starting transfers between devices  15.7 us (21%)
  waiting for transfers between devices  13.3 us (18%)
  other arithmetic  0.81 us (1%)
    all_to_all x1, blocking collectives, exchange(): lax.all_to_all(x, 'ctx', 0, 0, axis_index_groups=same_core, tiled=True)  17.4 us
    ppermute x11, starting transfers between devices, trade(): lax.ppermute(array, 'ctx', [(i, i ^ move) for i in range(devices)])  14.9 us
    pallas_call x1, Pallas kernels, feed_forward(): pl.pallas_call(feed_forward_kernel, out_shape=(pltpu.VMEM(near.shape, F32...  11.8 us
    pallas_call x4, Pallas kernels, load(): pl.pallas_call(functools.partial(load_kernel, starts=tuple((start for _,...  10.8 us
    ppermute x11, waiting for transfers between devices, trade(): lax.ppermute(array, 'ctx', [(i, i ^ move) for i in range(devices)])  10.4 us
    ppermute x4, waiting for transfers between devices, swap(): return lax.ppermute(x, 'ctx', partners)  2.93 us
    pallas_call x2, Pallas kernels, attend(): pl.pallas_call(attend_kernel, out_shape=pltpu.VMEM(q.shape, dtype), in_sp...  2.41 us
  transfers between devices with their start and end apart: 15, of which 9 were waited for; matrix products, arithmetic and copies ran while one was open for 0% of the time, Pallas kernels for 16%

profile of v4, /device:TPU:0, one launch (start us, length us, event | category | flops | bytes accessed | tf_op | source)
XLA Modules:
  0.0 74.8 jit_solution(10748725981802026304)
XLA Ops:
  0.0 0.9 %pack.1 = bf16[8,9,16,128]{3,2,1,0:T(8,128)(2,1)S(1)} custom-call(s32[2]{0:T(128)} %lengths_hbm.1, bf16[2,8192]{1,0:T(2,128)(2,1)} %q_hbm.1), custom_call_target="tpu_custom_call" | custom-call | tf_op jit(solution)/shard_map/pack/pallas_call | solution.py:69
  0.9 17.4 %all_to_all.5.q_ref = bf16[8,9,16,128]{3,2,1,0:T(8,128)(2,1)S(1)} all-to-all(bf16[8,9,16,128]{3,2,1,0:T(8,128)(2,1)S(1)} %pack.1), channel_id=1, replica_groups={{0,2,4,6,8,10,12,14},{1,3,5,7,9,11,13,15},{16,18,20,22,24,26,28,30},{17..., dimensions={0} | all-to-all | bytes 589824 | tf_op jit(solution)/shard_map/all_to_all | solution.py:415
  18.3 1.6 %load.4 = (bf16[512,1024]{1,0:T(8,128)(2,1)S(1)}, bf16[512,1024]{1,0:T(8,128)(2,1)S(1)}, s32[1,512]{1,0:T(1,128)S(1)}) custom-call(bf16[512,1024]{1,0:T(8,128)(2,1)} %refs_0_, bf16[512,1024]{1,0:T(8,128)(2,1)} %refs_1_.1, s32[1,512]{1,0:T(1,128)} %bitcast.3), custom_call_target="tpu_custom_call" | custom-call | bytes 2098176 | tf_op jit(solution)/shard_map/load/pallas_call | solution.py:101
  19.9 1.2 %attend.2 = bf16[8,9,16,128]{3,2,1,0:T(8,128)(2,1)S(1)} custom-call(bf16[8,9,16,128]{3,2,1,0:T(8,128)(2,1)S(1)} %collective-permute-done.q_ref, s32[1,512]{1,0:T(1,128)S(1)} %get-tuple-element.46.position_ref, bf16[512,1024]{1,0:T(8,128)(2,1)S(1)} %get-tuple-element.47.k_ref, bf16[512,1024]{1,0:T(8,128)(2,1)S(1)} %get-tuple-element.48.v_ref), custom_call_target="tpu_custom_call" | custom-call | flops 301989888 | bytes 2097152 | tf_op jit(solution)/shard_map/attend/pallas_call | solution.py:157
  21.1 0.6 collective-permute-start.1
  21.7 1.2 %attend.3.refs_0_ = f32[8,9,16,128]{3,2,1,0:T(8,128)S(1)} custom-call(bf16[8,9,16,128]{3,2,1,0:T(8,128)(2,1)S(1)} %all_to_all.5.q_ref, s32[1,512]{1,0:T(1,128)S(1)} %get-tuple-element.46.position_ref, bf16[512,1024]{1,0:T(8,128)(2,1)S(1)} %get-tuple-element.47.k_ref, bf16[512,1024]{1,0:T(8,128)(2,1)S(1)} %get-tuple-element.48.v_ref), custom_call_target="tpu_custom_call" | custom-call | flops 301989888 | bytes 2097152 | tf_op jit(solution)/shard_map/attend/pallas_call | solution.py:157
  22.9 0.6 combine.2
  23.5 0.7 collective-permute-start.2
  24.2 1.4 %collective-permute-start.3 = (bf16[2,9,16,128]{3,2,1,0:T(8,128)(2,1)S(1)}, bf16[2,9,16,128]{3,2,1,0:T(8,128)(2,1)S(1)}, u32[]{:S(2)}, u32[]{:S(2)}) collective-permute-start(bf16[2,9,16,128]{3,2,1,0:T(8,128)(2,1)S(1)} %get-tuple-element.56), channel_id=1, source_target_pairs={{0,4},{1,5},{2,6},{3,7},{4,0},{5,1},{6,2},{7,3},{8,12},{9,13},{10,... | collective-permute-start | bytes 221192 | tf_op jit(solution)/shard_map/ppermute | solution.py:388
  25.6 2.4 %collective-permute-start.4 = (bf16[2,9,16,128]{3,2,1,0:T(8,128)(2,1)S(1)}, bf16[2,9,16,128]{3,2,1,0:T(8,128)(2,1)S(1)}, u32[]{:S(2)}, u32[]{:S(2)}) collective-permute-start(bf16[2,9,16,128]{3,2,1,0:T(8,128)(2,1)S(1)} %get-tuple-element.57), channel_id=1, source_target_pairs={{0,12},{1,13},{2,14},{3,15},{4,8},{5,9},{6,10},{7,11},{8,4},{9,5},... | collective-permute-start | bytes 221192 | tf_op jit(solution)/shard_map/ppermute | solution.py:388
  27.9 3.1 %load.5.gate_a_ref = bf16[448,8192]{1,0:T(8,128)(2,1)S(1)} custom-call(bf16[896,8192]{1,0:T(8,128)(2,1)} %refs_0_.2), custom_call_target="tpu_custom_call" | custom-call | bytes 7340032 | tf_op jit(solution)/shard_map/load/pallas_call | solution.py:101
  31.3 1.1 %collective-permute-done.4.refs_3_ = bf16[2,9,16,128]{3,2,1,0:T(8,128)(2,1)S(1)} collective-permute-done((bf16[2,9,16,128]{3,2,1,0:T(8,128)(2,1)S(1)}, bf16[2,9,16,128]{3,2,1,0:T(8,128)(2,1)S(1)}, u32[]{:S(2)}, u32[]{:S(2)}) %collective-permute-start.4) | collective-permute-done | bytes 73760 | tf_op jit(solution)/shard_map/ppermute | solution.py:388
  32.6 0.5 collective-permute-start.5
  33.2 3.1 %load.6.gate_b_ref = bf16[448,8192]{1,0:T(8,128)(2,1)S(1)} custom-call(bf16[896,8192]{1,0:T(8,128)(2,1)} %refs_0_.2), custom_call_target="tpu_custom_call" | custom-call | bytes 7340032 | tf_op jit(solution)/shard_map/load/pallas_call | solution.py:101
  36.3 0.8 %collective-permute-done.5.came_ref = bf16[2,9,16,128]{3,2,1,0:T(8,128)(2,1)S(1)} collective-permute-done((bf16[2,9,16,128]{3,2,1,0:T(8,128)(2,1)S(1)}, bf16[2,9,16,128]{3,2,1,0:T(8,128)(2,1)S(1)}, u32[]{:S(2)}, u32[]{:S(2)}) %collective-permute-start.5) | collective-permute-done | bytes 73760 | tf_op jit(solution)/shard_map/ppermute | solution.py:388
  37.1 0.5 finish.1
  37.6 2.0 %collective-permute-start.6 = (bf16[4,8192]{1,0:T(4,128)(2,1)S(1)}, bf16[4,8192]{1,0:T(4,128)(2,1)S(1)}, u32[]{:S(2)}, u32[]{:S(2)}) collective-permute-start(bf16[4,8192]{1,0:T(4,128)(2,1)S(1)} %finish.1), channel_id=1, source_target_pairs={{0,8},{1,9},{2,10},{3,11},{4,12},{5,13},{6,14},{7,15},{8,0},{9,1},... | collective-permute-start | bytes 196616 | tf_op jit(solution)/shard_map/ppermute | solution.py:388
  39.6 0.4 collective-permute-start.7
  40.0 2.1 %collective-permute-start.8 = (bf16[4,8192]{1,0:T(4,128)(2,1)S(1)}, bf16[4,8192]{1,0:T(4,128)(2,1)S(1)}, u32[]{:S(2)}, u32[]{:S(2)}) collective-permute-start(bf16[4,8192]{1,0:T(4,128)(2,1)S(1)} %finish.1), channel_id=1, source_target_pairs={{0,12},{1,13},{2,14},{3,15},{4,8},{5,9},{6,10},{7,11},{8,4},{9,5},... | collective-permute-start | bytes 196616 | tf_op jit(solution)/shard_map/ppermute | solution.py:388
  42.0 3.1 %load.7.up_a_ref = bf16[448,8192]{1,0:T(8,128)(2,1)S(1)} custom-call(bf16[896,8192]{1,0:T(8,128)(2,1)} %up_hbm.1), custom_call_target="tpu_custom_call" | custom-call | bytes 7340032 | tf_op jit(solution)/shard_map/load/pallas_call | solution.py:101
  45.2 1.0 %collective-permute-done.8 = bf16[4,8192]{1,0:T(4,128)(2,1)S(1)} collective-permute-done((bf16[4,8192]{1,0:T(4,128)(2,1)S(1)}, bf16[4,8192]{1,0:T(4,128)(2,1)S(1)}, u32[]{:S(2)}, u32[]{:S(2)}) %collective-permute-start.8) | collective-permute-done | bytes 65568 | tf_op jit(solution)/shard_map/ppermute | solution.py:388
  46.4 1.5 %collective-permute-done.9.far_ref = bf16[16,8192]{1,0:T(8,128)(2,1)S(1)} collective-permute-done((bf16[16,8192]{1,0:T(8,128)(2,1)S(1)}, bf16[16,8192]{1,0:T(8,128)(2,1)S(1)}, u32[]{:S(2)}, u32[]{:S(2)}) %collective-permute-start.9) | collective-permute-done | bytes 262176 | tf_op jit(solution)/shard_map/ppermute | solution.py:418
  47.9 11.8 %feed_forward.1 = (f32[16,8192]{1,0:T(8,128)S(1)}, bf16[16,8192]{1,0:T(8,128)(2,1)S(1)}) custom-call(bf16[16,8192]{1,0:T(8,128)(2,1)S(1)} %pad_maximum_fusion.near_ref, bf16[16,8192]{1,0:T(8,128)(2,1)S(1)} %collective-permute-done.9.far_ref, bf16[448,8192]{1,0:T(8,128)(2,1)S(1)} %load.5.gate_a_ref, bf16[448,8192]{1,0:T(8,128)(2,1)S(1)} %load.6.gate_b_ref, ...), custom_call_target="tpu_custom_call" | custom-call | flops 1409286144 | bytes 22020096 | tf_op jit(solution)/shard_map/feed_forward/pallas_call | solution.py:316
  59.9 1.4 %collective-permute-done.10.refs_1_ = bf16[16,8192]{1,0:T(8,128)(2,1)S(1)} collective-permute-done((bf16[16,8192]{1,0:T(8,128)(2,1)S(1)}, bf16[16,8192]{1,0:T(8,128)(2,1)S(1)}, u32[]{:S(2)}, u32[]{:S(2)}) %collective-permute-start.10) | collective-permute-done | bytes 262176 | tf_op jit(solution)/shard_map/ppermute | solution.py:418
  61.4 1.4 %collective-permute-start.11 = (bf16[4,8192]{1,0:T(4,128)(2,1)S(1)}, bf16[4,8192]{1,0:T(4,128)(2,1)S(1)}, u32[]{:S(2)}, u32[]{:S(2)}) collective-permute-start(bf16[4,8192]{1,0:T(4,128)(2,1)S(1)} %get-tuple-element.78), channel_id=1, source_target_pairs={{0,8},{1,9},{2,10},{3,11},{4,12},{5,13},{6,14},{7,15},{8,0},{9,1},... | collective-permute-start | bytes 196616 | tf_op jit(solution)/shard_map/ppermute | solution.py:388
  62.8 1.3 %collective-permute-start.12 = (bf16[4,8192]{1,0:T(4,128)(2,1)S(1)}, bf16[4,8192]{1,0:T(4,128)(2,1)S(1)}, u32[]{:S(2)}, u32[]{:S(2)}) collective-permute-start(bf16[4,8192]{1,0:T(4,128)(2,1)S(1)} %get-tuple-element.79), channel_id=1, source_target_pairs={{0,4},{1,5},{2,6},{3,7},{4,0},{5,1},{6,2},{7,3},{8,12},{9,13},{10,... | collective-permute-start | bytes 196616 | tf_op jit(solution)/shard_map/ppermute | solution.py:388
  64.1 1.7 %collective-permute-start.13 = (bf16[4,8192]{1,0:T(4,128)(2,1)S(1)}, bf16[4,8192]{1,0:T(4,128)(2,1)S(1)}, u32[]{:S(2)}, u32[]{:S(2)}) collective-permute-start(bf16[4,8192]{1,0:T(4,128)(2,1)S(1)} %get-tuple-element.80), channel_id=1, source_target_pairs={{0,12},{1,13},{2,14},{3,15},{4,8},{5,9},{6,10},{7,11},{8,4},{9,5},... | collective-permute-start | bytes 196616 | tf_op jit(solution)/shard_map/ppermute | solution.py:388
  65.8 3.3 %collective-permute-done.11.refs_1_ = bf16[4,8192]{1,0:T(4,128)(2,1)S(1)} collective-permute-done((bf16[4,8192]{1,0:T(4,128)(2,1)S(1)}, bf16[4,8192]{1,0:T(4,128)(2,1)S(1)}, u32[]{:S(2)}, u32[]{:S(2)}) %collective-permute-start.11) | collective-permute-done | bytes 65568 | tf_op jit(solution)/shard_map/ppermute | solution.py:388
  69.1 1.0 %collective-permute-done.13.refs_3_ = bf16[4,8192]{1,0:T(4,128)(2,1)S(1)} collective-permute-done((bf16[4,8192]{1,0:T(4,128)(2,1)S(1)}, bf16[4,8192]{1,0:T(4,128)(2,1)S(1)}, u32[]{:S(2)}, u32[]{:S(2)}) %collective-permute-start.13) | collective-permute-done | bytes 65568 | tf_op jit(solution)/shard_map/ppermute | solution.py:388
  70.2 1.0 %collective-permute-start.14 = (bf16[2,8192]{1,0:T(2,128)(2,1)S(1)}, bf16[2,8192]{1,0:T(2,128)(2,1)S(1)}, u32[]{:S(2)}, u32[]{:S(2)}) collective-permute-start(bf16[2,8192]{1,0:T(2,128)(2,1)S(1)} %get-tuple-element.82), channel_id=1, source_target_pairs={{0,2},{1,3},{2,0},{3,1},{4,6},{5,7},{6,4},{7,5},{8,10},{9,11},{10,... | collective-permute-start | bytes 98312 | tf_op jit(solution)/shard_map/ppermute | solution.py:388
  71.2 3.0 %collective-permute-done.14 = bf16[2,8192]{1,0:T(2,128)(2,1)S(1)} collective-permute-done((bf16[2,8192]{1,0:T(2,128)(2,1)S(1)}, bf16[2,8192]{1,0:T(2,128)(2,1)S(1)}, u32[]{:S(2)}, u32[]{:S(2)}) %collective-permute-start.14) | collective-permute-done | bytes 32800 | tf_op jit(solution)/shard_map/ppermute | solution.py:388
  74.2 0.6 add_convert_fusion
  (16 shorter events, 1.1 us)
Async XLA Ops:
  18.3 1.6 %collective-permute-start = (bf16[8,9,16,128]{3,2,1,0:T(8,128)(2,1)S(1)}, bf16[8,9,16,128]{3,2,1,0:T(8,128)(2,1)S(1)}, u32[]{:S(2)}, u32[]{:S(2)}) collective-permute-start(bf16[8,9,16,128]{3,2,1,0:T(8,128)(2,1)S(1)} %all_to_all.5.q_ref), channel_id=1, source_target_pairs={{0,1},{1,0},{2,3},{3,2},{4,5},{5,4},{6,7},{7,6},{8,9},{9,8},{10,11... | collective-permute-start | bytes 884744 | tf_op jit(solution)/shard_map/ppermute | solution.py:418
  21.1 1.8 %collective-permute-start.1 = (bf16[8,9,16,128]{3,2,1,0:T(8,128)(2,1)S(1)}, bf16[8,9,16,128]{3,2,1,0:T(8,128)(2,1)S(1)}, u32[]{:S(2)}, u32[]{:S(2)}) collective-permute-start(bf16[8,9,16,128]{3,2,1,0:T(8,128)(2,1)S(1)} %attend.2), channel_id=1, source_target_pairs={{0,1},{1,0},{2,3},{3,2},{4,5},{5,4},{6,7},{7,6},{8,9},{9,8},{10,11... | collective-permute-start | bytes 884744 | tf_op jit(solution)/shard_map/ppermute | solution.py:418
  23.5 7.8 %collective-permute-start.2 = (bf16[2,9,16,128]{3,2,1,0:T(8,128)(2,1)S(1)}, bf16[2,9,16,128]{3,2,1,0:T(8,128)(2,1)S(1)}, u32[]{:S(2)}, u32[]{:S(2)}) collective-permute-start(bf16[2,9,16,128]{3,2,1,0:T(8,128)(2,1)S(1)} %get-tuple-element.55), channel_id=1, source_target_pairs={{0,8},{1,9},{2,10},{3,11},{4,12},{5,13},{6,14},{7,15},{8,0},{9,1},... | collective-permute-start | bytes 221192 | tf_op jit(solution)/shard_map/ppermute | solution.py:388
  24.2 7.1 %collective-permute-start.3 = (bf16[2,9,16,128]{3,2,1,0:T(8,128)(2,1)S(1)}, bf16[2,9,16,128]{3,2,1,0:T(8,128)(2,1)S(1)}, u32[]{:S(2)}, u32[]{:S(2)}) collective-permute-start(bf16[2,9,16,128]{3,2,1,0:T(8,128)(2,1)S(1)} %get-tuple-element.56), channel_id=1, source_target_pairs={{0,4},{1,5},{2,6},{3,7},{4,0},{5,1},{6,2},{7,3},{8,12},{9,13},{10,... | collective-permute-start | bytes 221192 | tf_op jit(solution)/shard_map/ppermute | solution.py:388
  25.6 6.8 %collective-permute-start.4 = (bf16[2,9,16,128]{3,2,1,0:T(8,128)(2,1)S(1)}, bf16[2,9,16,128]{3,2,1,0:T(8,128)(2,1)S(1)}, u32[]{:S(2)}, u32[]{:S(2)}) collective-permute-start(bf16[2,9,16,128]{3,2,1,0:T(8,128)(2,1)S(1)} %get-tuple-element.57), channel_id=1, source_target_pairs={{0,12},{1,13},{2,14},{3,15},{4,8},{5,9},{6,10},{7,11},{8,4},{9,5},... | collective-permute-start | bytes 221192 | tf_op jit(solution)/shard_map/ppermute | solution.py:388
  31.0 6.0 %copy-start = (f32[8192]{0:T(1024)S(1)}, f32[8192]{0:T(1024)}, u32[]{:S(2)}) copy-start(f32[8192]{0:T(1024)} %param.14) | copy-start | bytes 98308
  32.6 4.4 %collective-permute-start.5 = (bf16[2,9,16,128]{3,2,1,0:T(8,128)(2,1)S(1)}, bf16[2,9,16,128]{3,2,1,0:T(8,128)(2,1)S(1)}, u32[]{:S(2)}, u32[]{:S(2)}) collective-permute-start(bf16[2,9,16,128]{3,2,1,0:T(8,128)(2,1)S(1)} %combine.3.mine_ref), channel_id=1, source_target_pairs={{0,2},{1,3},{2,0},{3,1},{4,6},{5,7},{6,4},{7,5},{8,10},{9,11},{10,... | collective-permute-start | bytes 221192 | tf_op jit(solution)/shard_map/ppermute | solution.py:388
  37.6 7.6 %collective-permute-start.6 = (bf16[4,8192]{1,0:T(4,128)(2,1)S(1)}, bf16[4,8192]{1,0:T(4,128)(2,1)S(1)}, u32[]{:S(2)}, u32[]{:S(2)}) collective-permute-start(bf16[4,8192]{1,0:T(4,128)(2,1)S(1)} %finish.1), channel_id=1, source_target_pairs={{0,8},{1,9},{2,10},{3,11},{4,12},{5,13},{6,14},{7,15},{8,0},{9,1},... | collective-permute-start | bytes 196616 | tf_op jit(solution)/shard_map/ppermute | solution.py:388
  39.6 5.6 %collective-permute-start.7 = (bf16[4,8192]{1,0:T(4,128)(2,1)S(1)}, bf16[4,8192]{1,0:T(4,128)(2,1)S(1)}, u32[]{:S(2)}, u32[]{:S(2)}) collective-permute-start(bf16[4,8192]{1,0:T(4,128)(2,1)S(1)} %finish.1), channel_id=1, source_target_pairs={{0,4},{1,5},{2,6},{3,7},{4,0},{5,1},{6,2},{7,3},{8,12},{9,13},{10,... | collective-permute-start | bytes 196616 | tf_op jit(solution)/shard_map/ppermute | solution.py:388
  40.0 6.2 %collective-permute-start.8 = (bf16[4,8192]{1,0:T(4,128)(2,1)S(1)}, bf16[4,8192]{1,0:T(4,128)(2,1)S(1)}, u32[]{:S(2)}, u32[]{:S(2)}) collective-permute-start(bf16[4,8192]{1,0:T(4,128)(2,1)S(1)} %finish.1), channel_id=1, source_target_pairs={{0,12},{1,13},{2,14},{3,15},{4,8},{5,9},{6,10},{7,11},{8,4},{9,5},... | collective-permute-start | bytes 196616 | tf_op jit(solution)/shard_map/ppermute | solution.py:388
  46.3 1.6 %collective-permute-start.9 = (bf16[16,8192]{1,0:T(8,128)(2,1)S(1)}, bf16[16,8192]{1,0:T(8,128)(2,1)S(1)}, u32[]{:S(2)}, u32[]{:S(2)}) collective-permute-start(bf16[16,8192]{1,0:T(8,128)(2,1)S(1)} %pad_maximum_fusion.near_ref), channel_id=1, source_target_pairs={{0,1},{1,0},{2,3},{3,2},{4,5},{5,4},{6,7},{7,6},{8,9},{9,8},{10,11... | collective-permute-start | bytes 786440 | tf_op jit(solution)/shard_map/ppermute | solution.py:418
  59.7 1.6 %collective-permute-start.10 = (bf16[16,8192]{1,0:T(8,128)(2,1)S(1)}, bf16[16,8192]{1,0:T(8,128)(2,1)S(1)}, u32[]{:S(2)}, u32[]{:S(2)}) collective-permute-start(bf16[16,8192]{1,0:T(8,128)(2,1)S(1)} %get-tuple-element.76), channel_id=1, source_target_pairs={{0,1},{1,0},{2,3},{3,2},{4,5},{5,4},{6,7},{7,6},{8,9},{9,8},{10,11... | collective-permute-start | bytes 786440 | tf_op jit(solution)/shard_map/ppermute | solution.py:418
  61.4 7.7 %collective-permute-start.11 = (bf16[4,8192]{1,0:T(4,128)(2,1)S(1)}, bf16[4,8192]{1,0:T(4,128)(2,1)S(1)}, u32[]{:S(2)}, u32[]{:S(2)}) collective-permute-start(bf16[4,8192]{1,0:T(4,128)(2,1)S(1)} %get-tuple-element.78), channel_id=1, source_target_pairs={{0,8},{1,9},{2,10},{3,11},{4,12},{5,13},{6,14},{7,15},{8,0},{9,1},... | collective-permute-start | bytes 196616 | tf_op jit(solution)/shard_map/ppermute | solution.py:388
  62.8 6.3 %collective-permute-start.12 = (bf16[4,8192]{1,0:T(4,128)(2,1)S(1)}, bf16[4,8192]{1,0:T(4,128)(2,1)S(1)}, u32[]{:S(2)}, u32[]{:S(2)}) collective-permute-start(bf16[4,8192]{1,0:T(4,128)(2,1)S(1)} %get-tuple-element.79), channel_id=1, source_target_pairs={{0,4},{1,5},{2,6},{3,7},{4,0},{5,1},{6,2},{7,3},{8,12},{9,13},{10,... | collective-permute-start | bytes 196616 | tf_op jit(solution)/shard_map/ppermute | solution.py:388
  64.1 6.1 %collective-permute-start.13 = (bf16[4,8192]{1,0:T(4,128)(2,1)S(1)}, bf16[4,8192]{1,0:T(4,128)(2,1)S(1)}, u32[]{:S(2)}, u32[]{:S(2)}) collective-permute-start(bf16[4,8192]{1,0:T(4,128)(2,1)S(1)} %get-tuple-element.80), channel_id=1, source_target_pairs={{0,12},{1,13},{2,14},{3,15},{4,8},{5,9},{6,10},{7,11},{8,4},{9,5},... | collective-permute-start | bytes 196616 | tf_op jit(solution)/shard_map/ppermute | solution.py:388
  70.2 4.0 %collective-permute-start.14 = (bf16[2,8192]{1,0:T(2,128)(2,1)S(1)}, bf16[2,8192]{1,0:T(2,128)(2,1)S(1)}, u32[]{:S(2)}, u32[]{:S(2)}) collective-permute-start(bf16[2,8192]{1,0:T(2,128)(2,1)S(1)} %get-tuple-element.82), channel_id=1, source_target_pairs={{0,2},{1,3},{2,0},{3,1},{4,6},{5,7},{6,4},{7,5},{8,10},{9,11},{10,... | collective-permute-start | bytes 98312 | tf_op jit(solution)/shard_map/ppermute | solution.py:388

commit v5 on v4

--- a/solution.py
+++ b/solution.py
@@ -1,5 +1,4 @@
 import functools
-import math
 
 import jax
 import jax.numpy as jnp
@@ -15,7 +14,7 @@
 GROUP = QUERY_HEADS // KEY_VALUE_HEADS
 F32 = jnp.float32
 BF16 = jnp.bfloat16
-SCALE = HEAD_SIZE ** (-0.5) * math.log2(math.e)
+SCALE = HEAD_SIZE ** (-0.5)
 DEAD = -1e30
 ROWS_BY_ROWS = (((1,), (1,)), ((), ()))
 VMEM = pl.BlockSpec(memory_space=pltpu.VMEM)
@@ -140,7 +139,7 @@
         if g + 1 < KEY_VALUE_HEADS:
             coming = score(g + 1)
         peak = rounded(jnp.maximum(jnp.max(scores, axis=1, keepdims=True), 0.1 * DEAD))
-        weights = jnp.exp2(scores - peak)
+        weights = jnp.exp(scores - peak)
         total = jnp.sum(weights, axis=1, keepdims=True)
         if waiting is not None:
             add_up(g - 1, waiting)
@@ -170,7 +169,7 @@
 def joined(states):
     lane = lax.broadcasted_iota(jnp.int32, states[0].shape, 1)
     peak = functools.reduce(jnp.maximum, states)
-    scales = [jnp.exp2(state - peak) for state in states]
+    scales = [jnp.exp(state - peak) for state in states]
     total = jnp.zeros_like(peak)
     for state, scale in zip(states, scales):
         high = jnp.where(lane < 2 * KEY_VALUE_HEADS, state, 0.0)

time: 75.2 us -> 75.2 us (level)
  no operation moved by 1% of the time
where the time goes in v5:
time: 75.2 us; the launch traced here: 74.9 us
  Pallas kernels  27.5 us (37%)
  blocking collectives  17.4 us (23%)
  starting transfers between devices  15.7 us (21%)
  waiting for transfers between devices  13.3 us (18%)
  other arithmetic  0.81 us (1%)
    all_to_all x1, blocking collectives, exchange(): lax.all_to_all(x, 'ctx', 0, 0, axis_index_groups=same_core, tiled=True)  17.4 us
    ppermute x11, starting transfers between devices, trade(): lax.ppermute(array, 'ctx', [(i, i ^ move) for i in range(devices)])  14.9 us
    pallas_call x1, Pallas kernels, feed_forward(): pl.pallas_call(feed_forward_kernel, out_shape=(pltpu.VMEM(near.shape, F32...  11.8 us
    pallas_call x4, Pallas kernels, load(): pl.pallas_call(functools.partial(load_kernel, starts=tuple((start for _,...  10.8 us
    ppermute x11, waiting for transfers between devices, trade(): lax.ppermute(array, 'ctx', [(i, i ^ move) for i in range(devices)])  10.3 us
    ppermute x4, waiting for transfers between devices, swap(): return lax.ppermute(x, 'ctx', partners)  2.92 us
    pallas_call x2, Pallas kernels, attend(): pl.pallas_call(attend_kernel, out_shape=pltpu.VMEM(q.shape, dtype), in_sp...  2.49 us
  transfers between devices with their start and end apart: 15, of which 9 were waited for; matrix products, arithmetic and copies ran while one was open for 0% of the time, Pallas kernels for 16%

profile of v5, /device:TPU:0, one launch (start us, length us, event | category | flops | bytes accessed | tf_op | source)
XLA Modules:
  0.0 74.9 jit_solution(6273995951248575837)
XLA Ops:
  0.0 0.9 %pack.1 = bf16[8,9,16,128]{3,2,1,0:T(8,128)(2,1)S(1)} custom-call(s32[2]{0:T(128)} %lengths_hbm.1, bf16[2,8192]{1,0:T(2,128)(2,1)} %q_hbm.1), custom_call_target="tpu_custom_call" | custom-call | tf_op jit(solution)/shard_map/pack/pallas_call | solution.py:68
  0.9 17.4 %all_to_all.5.q_ref = bf16[8,9,16,128]{3,2,1,0:T(8,128)(2,1)S(1)} all-to-all(bf16[8,9,16,128]{3,2,1,0:T(8,128)(2,1)S(1)} %pack.1), channel_id=1, replica_groups={{0,2,4,6,8,10,12,14},{1,3,5,7,9,11,13,15},{16,18,20,22,24,26,28,30},{17..., dimensions={0} | all-to-all | bytes 589824 | tf_op jit(solution)/shard_map/all_to_all | solution.py:414
  18.3 1.6 %load.4 = (bf16[512,1024]{1,0:T(8,128)(2,1)S(1)}, bf16[512,1024]{1,0:T(8,128)(2,1)S(1)}, s32[1,512]{1,0:T(1,128)S(1)}) custom-call(bf16[512,1024]{1,0:T(8,128)(2,1)} %refs_0_, bf16[512,1024]{1,0:T(8,128)(2,1)} %refs_1_.1, s32[1,512]{1,0:T(1,128)} %bitcast.3), custom_call_target="tpu_custom_call" | custom-call | bytes 2098176 | tf_op jit(solution)/shard_map/load/pallas_call | solution.py:100
  19.9 1.2 %attend.2 = bf16[8,9,16,128]{3,2,1,0:T(8,128)(2,1)S(1)} custom-call(bf16[8,9,16,128]{3,2,1,0:T(8,128)(2,1)S(1)} %collective-permute-done.q_ref, s32[1,512]{1,0:T(1,128)S(1)} %get-tuple-element.46.position_ref, bf16[512,1024]{1,0:T(8,128)(2,1)S(1)} %get-tuple-element.47.k_ref, bf16[512,1024]{1,0:T(8,128)(2,1)S(1)} %get-tuple-element.48.v_ref), custom_call_target="tpu_custom_call" | custom-call | flops 301989888 | bytes 2097152 | tf_op jit(solution)/shard_map/attend/pallas_call | solution.py:156
  21.2 0.6 collective-permute-start.1
  21.7 1.2 %attend.3.refs_0_ = f32[8,9,16,128]{3,2,1,0:T(8,128)S(1)} custom-call(bf16[8,9,16,128]{3,2,1,0:T(8,128)(2,1)S(1)} %all_to_all.5.q_ref, s32[1,512]{1,0:T(1,128)S(1)} %get-tuple-element.46.position_ref, bf16[512,1024]{1,0:T(8,128)(2,1)S(1)} %get-tuple-element.47.k_ref, bf16[512,1024]{1,0:T(8,128)(2,1)S(1)} %get-tuple-element.48.v_ref), custom_call_target="tpu_custom_call" | custom-call | flops 301989888 | bytes 2097152 | tf_op jit(solution)/shard_map/attend/pallas_call | solution.py:156
  23.0 0.6 combine.2
  23.6 0.7 collective-permute-start.2
  24.3 1.4 %collective-permute-start.3 = (bf16[2,9,16,128]{3,2,1,0:T(8,128)(2,1)S(1)}, bf16[2,9,16,128]{3,2,1,0:T(8,128)(2,1)S(1)}, u32[]{:S(2)}, u32[]{:S(2)}) collective-permute-start(bf16[2,9,16,128]{3,2,1,0:T(8,128)(2,1)S(1)} %get-tuple-element.56), channel_id=1, source_target_pairs={{0,4},{1,5},{2,6},{3,7},{4,0},{5,1},{6,2},{7,3},{8,12},{9,13},{10,... | collective-permute-start | bytes 221192 | tf_op jit(solution)/shard_map/ppermute | solution.py:387
  25.6 2.4 %collective-permute-start.4 = (bf16[2,9,16,128]{3,2,1,0:T(8,128)(2,1)S(1)}, bf16[2,9,16,128]{3,2,1,0:T(8,128)(2,1)S(1)}, u32[]{:S(2)}, u32[]{:S(2)}) collective-permute-start(bf16[2,9,16,128]{3,2,1,0:T(8,128)(2,1)S(1)} %get-tuple-element.57), channel_id=1, source_target_pairs={{0,12},{1,13},{2,14},{3,15},{4,8},{5,9},{6,10},{7,11},{8,4},{9,5},... | collective-permute-start | bytes 221192 | tf_op jit(solution)/shard_map/ppermute | solution.py:387
  28.0 3.1 %load.5.gate_a_ref = bf16[448,8192]{1,0:T(8,128)(2,1)S(1)} custom-call(bf16[896,8192]{1,0:T(8,128)(2,1)} %refs_0_.2), custom_call_target="tpu_custom_call" | custom-call | bytes 7340032 | tf_op jit(solution)/shard_map/load/pallas_call | solution.py:100
  31.3 1.1 %collective-permute-done.4.refs_3_ = bf16[2,9,16,128]{3,2,1,0:T(8,128)(2,1)S(1)} collective-permute-done((bf16[2,9,16,128]{3,2,1,0:T(8,128)(2,1)S(1)}, bf16[2,9,16,128]{3,2,1,0:T(8,128)(2,1)S(1)}, u32[]{:S(2)}, u32[]{:S(2)}) %collective-permute-start.4) | collective-permute-done | bytes 73760 | tf_op jit(solution)/shard_map/ppermute | solution.py:387
  32.7 0.5 collective-permute-start.5
  33.2 3.1 %load.6.gate_b_ref = bf16[448,8192]{1,0:T(8,128)(2,1)S(1)} custom-call(bf16[896,8192]{1,0:T(8,128)(2,1)} %refs_0_.2), custom_call_target="tpu_custom_call" | custom-call | bytes 7340032 | tf_op jit(solution)/shard_map/load/pallas_call | solution.py:100
  36.3 0.8 %collective-permute-done.5.came_ref = bf16[2,9,16,128]{3,2,1,0:T(8,128)(2,1)S(1)} collective-permute-done((bf16[2,9,16,128]{3,2,1,0:T(8,128)(2,1)S(1)}, bf16[2,9,16,128]{3,2,1,0:T(8,128)(2,1)S(1)}, u32[]{:S(2)}, u32[]{:S(2)}) %collective-permute-start.5) | collective-permute-done | bytes 73760 | tf_op jit(solution)/shard_map/ppermute | solution.py:387
  37.1 0.5 finish.1
  37.6 2.0 %collective-permute-start.6 = (bf16[4,8192]{1,0:T(4,128)(2,1)S(1)}, bf16[4,8192]{1,0:T(4,128)(2,1)S(1)}, u32[]{:S(2)}, u32[]{:S(2)}) collective-permute-start(bf16[4,8192]{1,0:T(4,128)(2,1)S(1)} %finish.1), channel_id=1, source_target_pairs={{0,8},{1,9},{2,10},{3,11},{4,12},{5,13},{6,14},{7,15},{8,0},{9,1},... | collective-permute-start | bytes 196616 | tf_op jit(solution)/shard_map/ppermute | solution.py:387
  39.6 0.4 collective-permute-start.7
  40.0 2.1 %collective-permute-start.8 = (bf16[4,8192]{1,0:T(4,128)(2,1)S(1)}, bf16[4,8192]{1,0:T(4,128)(2,1)S(1)}, u32[]{:S(2)}, u32[]{:S(2)}) collective-permute-start(bf16[4,8192]{1,0:T(4,128)(2,1)S(1)} %finish.1), channel_id=1, source_target_pairs={{0,12},{1,13},{2,14},{3,15},{4,8},{5,9},{6,10},{7,11},{8,4},{9,5},... | collective-permute-start | bytes 196616 | tf_op jit(solution)/shard_map/ppermute | solution.py:387
  42.1 3.1 %load.7.up_a_ref = bf16[448,8192]{1,0:T(8,128)(2,1)S(1)} custom-call(bf16[896,8192]{1,0:T(8,128)(2,1)} %up_hbm.1), custom_call_target="tpu_custom_call" | custom-call | bytes 7340032 | tf_op jit(solution)/shard_map/load/pallas_call | solution.py:100
  45.2 1.0 %collective-permute-done.8 = bf16[4,8192]{1,0:T(4,128)(2,1)S(1)} collective-permute-done((bf16[4,8192]{1,0:T(4,128)(2,1)S(1)}, bf16[4,8192]{1,0:T(4,128)(2,1)S(1)}, u32[]{:S(2)}, u32[]{:S(2)}) %collective-permute-start.8) | collective-permute-done | bytes 65568 | tf_op jit(solution)/shard_map/ppermute | solution.py:387
  46.4 1.5 %collective-permute-done.9.far_ref = bf16[16,8192]{1,0:T(8,128)(2,1)S(1)} collective-permute-done((bf16[16,8192]{1,0:T(8,128)(2,1)S(1)}, bf16[16,8192]{1,0:T(8,128)(2,1)S(1)}, u32[]{:S(2)}, u32[]{:S(2)}) %collective-permute-start.9) | collective-permute-done | bytes 262176 | tf_op jit(solution)/shard_map/ppermute | solution.py:417
  48.0 11.8 %feed_forward.1 = (f32[16,8192]{1,0:T(8,128)S(1)}, bf16[16,8192]{1,0:T(8,128)(2,1)S(1)}) custom-call(bf16[16,8192]{1,0:T(8,128)(2,1)S(1)} %pad_maximum_fusion.near_ref, bf16[16,8192]{1,0:T(8,128)(2,1)S(1)} %collective-permute-done.9.far_ref, bf16[448,8192]{1,0:T(8,128)(2,1)S(1)} %load.5.gate_a_ref, bf16[448,8192]{1,0:T(8,128)(2,1)S(1)} %load.6.gate_b_ref, ...), custom_call_target="tpu_custom_call" | custom-call | flops 1409286144 | bytes 22020096 | tf_op jit(solution)/shard_map/feed_forward/pallas_call | solution.py:315
  60.0 1.4 %collective-permute-done.10.refs_1_ = bf16[16,8192]{1,0:T(8,128)(2,1)S(1)} collective-permute-done((bf16[16,8192]{1,0:T(8,128)(2,1)S(1)}, bf16[16,8192]{1,0:T(8,128)(2,1)S(1)}, u32[]{:S(2)}, u32[]{:S(2)}) %collective-permute-start.10) | collective-permute-done | bytes 262176 | tf_op jit(solution)/shard_map/ppermute | solution.py:417
  61.5 1.4 %collective-permute-start.11 = (bf16[4,8192]{1,0:T(4,128)(2,1)S(1)}, bf16[4,8192]{1,0:T(4,128)(2,1)S(1)}, u32[]{:S(2)}, u32[]{:S(2)}) collective-permute-start(bf16[4,8192]{1,0:T(4,128)(2,1)S(1)} %get-tuple-element.78), channel_id=1, source_target_pairs={{0,8},{1,9},{2,10},{3,11},{4,12},{5,13},{6,14},{7,15},{8,0},{9,1},... | collective-permute-start | bytes 196616 | tf_op jit(solution)/shard_map/ppermute | solution.py:387
  62.8 1.3 %collective-permute-start.12 = (bf16[4,8192]{1,0:T(4,128)(2,1)S(1)}, bf16[4,8192]{1,0:T(4,128)(2,1)S(1)}, u32[]{:S(2)}, u32[]{:S(2)}) collective-permute-start(bf16[4,8192]{1,0:T(4,128)(2,1)S(1)} %get-tuple-element.79), channel_id=1, source_target_pairs={{0,4},{1,5},{2,6},{3,7},{4,0},{5,1},{6,2},{7,3},{8,12},{9,13},{10,... | collective-permute-start | bytes 196616 | tf_op jit(solution)/shard_map/ppermute | solution.py:387
  64.1 1.8 %collective-permute-start.13 = (bf16[4,8192]{1,0:T(4,128)(2,1)S(1)}, bf16[4,8192]{1,0:T(4,128)(2,1)S(1)}, u32[]{:S(2)}, u32[]{:S(2)}) collective-permute-start(bf16[4,8192]{1,0:T(4,128)(2,1)S(1)} %get-tuple-element.80), channel_id=1, source_target_pairs={{0,12},{1,13},{2,14},{3,15},{4,8},{5,9},{6,10},{7,11},{8,4},{9,5},... | collective-permute-start | bytes 196616 | tf_op jit(solution)/shard_map/ppermute | solution.py:387
  65.9 3.2 %collective-permute-done.11.refs_1_ = bf16[4,8192]{1,0:T(4,128)(2,1)S(1)} collective-permute-done((bf16[4,8192]{1,0:T(4,128)(2,1)S(1)}, bf16[4,8192]{1,0:T(4,128)(2,1)S(1)}, u32[]{:S(2)}, u32[]{:S(2)}) %collective-permute-start.11) | collective-permute-done | bytes 65568 | tf_op jit(solution)/shard_map/ppermute | solution.py:387
  69.2 1.0 %collective-permute-done.13.refs_3_ = bf16[4,8192]{1,0:T(4,128)(2,1)S(1)} collective-permute-done((bf16[4,8192]{1,0:T(4,128)(2,1)S(1)}, bf16[4,8192]{1,0:T(4,128)(2,1)S(1)}, u32[]{:S(2)}, u32[]{:S(2)}) %collective-permute-start.13) | collective-permute-done | bytes 65568 | tf_op jit(solution)/shard_map/ppermute | solution.py:387
  70.3 1.0 %collective-permute-start.14 = (bf16[2,8192]{1,0:T(2,128)(2,1)S(1)}, bf16[2,8192]{1,0:T(2,128)(2,1)S(1)}, u32[]{:S(2)}, u32[]{:S(2)}) collective-permute-start(bf16[2,8192]{1,0:T(2,128)(2,1)S(1)} %get-tuple-element.82), channel_id=1, source_target_pairs={{0,2},{1,3},{2,0},{3,1},{4,6},{5,7},{6,4},{7,5},{8,10},{9,11},{10,... | collective-permute-start | bytes 98312 | tf_op jit(solution)/shard_map/ppermute | solution.py:387
  71.3 3.0 %collective-permute-done.14 = bf16[2,8192]{1,0:T(2,128)(2,1)S(1)} collective-permute-done((bf16[2,8192]{1,0:T(2,128)(2,1)S(1)}, bf16[2,8192]{1,0:T(2,128)(2,1)S(1)}, u32[]{:S(2)}, u32[]{:S(2)}) %collective-permute-start.14) | collective-permute-done | bytes 32800 | tf_op jit(solution)/shard_map/ppermute | solution.py:387
  74.2 0.6 add_convert_fusion
  (16 shorter events, 1.1 us)
Async XLA Ops:
  18.3 1.6 %collective-permute-start = (bf16[8,9,16,128]{3,2,1,0:T(8,128)(2,1)S(1)}, bf16[8,9,16,128]{3,2,1,0:T(8,128)(2,1)S(1)}, u32[]{:S(2)}, u32[]{:S(2)}) collective-permute-start(bf16[8,9,16,128]{3,2,1,0:T(8,128)(2,1)S(1)} %all_to_all.5.q_ref), channel_id=1, source_target_pairs={{0,1},{1,0},{2,3},{3,2},{4,5},{5,4},{6,7},{7,6},{8,9},{9,8},{10,11... | collective-permute-start | bytes 884744 | tf_op jit(solution)/shard_map/ppermute | solution.py:417
  21.2 1.8 %collective-permute-start.1 = (bf16[8,9,16,128]{3,2,1,0:T(8,128)(2,1)S(1)}, bf16[8,9,16,128]{3,2,1,0:T(8,128)(2,1)S(1)}, u32[]{:S(2)}, u32[]{:S(2)}) collective-permute-start(bf16[8,9,16,128]{3,2,1,0:T(8,128)(2,1)S(1)} %attend.2), channel_id=1, source_target_pairs={{0,1},{1,0},{2,3},{3,2},{4,5},{5,4},{6,7},{7,6},{8,9},{9,8},{10,11... | collective-permute-start | bytes 884744 | tf_op jit(solution)/shard_map/ppermute | solution.py:417
  23.6 7.8 %collective-permute-start.2 = (bf16[2,9,16,128]{3,2,1,0:T(8,128)(2,1)S(1)}, bf16[2,9,16,128]{3,2,1,0:T(8,128)(2,1)S(1)}, u32[]{:S(2)}, u32[]{:S(2)}) collective-permute-start(bf16[2,9,16,128]{3,2,1,0:T(8,128)(2,1)S(1)} %get-tuple-element.55), channel_id=1, source_target_pairs={{0,8},{1,9},{2,10},{3,11},{4,12},{5,13},{6,14},{7,15},{8,0},{9,1},... | collective-permute-start | bytes 221192 | tf_op jit(solution)/shard_map/ppermute | solution.py:387
  24.3 7.0 %collective-permute-start.3 = (bf16[2,9,16,128]{3,2,1,0:T(8,128)(2,1)S(1)}, bf16[2,9,16,128]{3,2,1,0:T(8,128)(2,1)S(1)}, u32[]{:S(2)}, u32[]{:S(2)}) collective-permute-start(bf16[2,9,16,128]{3,2,1,0:T(8,128)(2,1)S(1)} %get-tuple-element.56), channel_id=1, source_target_pairs={{0,4},{1,5},{2,6},{3,7},{4,0},{5,1},{6,2},{7,3},{8,12},{9,13},{10,... | collective-permute-start | bytes 221192 | tf_op jit(solution)/shard_map/ppermute | solution.py:387
  25.6 6.8 %collective-permute-start.4 = (bf16[2,9,16,128]{3,2,1,0:T(8,128)(2,1)S(1)}, bf16[2,9,16,128]{3,2,1,0:T(8,128)(2,1)S(1)}, u32[]{:S(2)}, u32[]{:S(2)}) collective-permute-start(bf16[2,9,16,128]{3,2,1,0:T(8,128)(2,1)S(1)} %get-tuple-element.57), channel_id=1, source_target_pairs={{0,12},{1,13},{2,14},{3,15},{4,8},{5,9},{6,10},{7,11},{8,4},{9,5},... | collective-permute-start | bytes 221192 | tf_op jit(solution)/shard_map/ppermute | solution.py:387
  31.1 6.0 %copy-start = (f32[8192]{0:T(1024)S(1)}, f32[8192]{0:T(1024)}, u32[]{:S(2)}) copy-start(f32[8192]{0:T(1024)} %param.14) | copy-start | bytes 98308
  32.7 4.4 %collective-permute-start.5 = (bf16[2,9,16,128]{3,2,1,0:T(8,128)(2,1)S(1)}, bf16[2,9,16,128]{3,2,1,0:T(8,128)(2,1)S(1)}, u32[]{:S(2)}, u32[]{:S(2)}) collective-permute-start(bf16[2,9,16,128]{3,2,1,0:T(8,128)(2,1)S(1)} %combine.3.mine_ref), channel_id=1, source_target_pairs={{0,2},{1,3},{2,0},{3,1},{4,6},{5,7},{6,4},{7,5},{8,10},{9,11},{10,... | collective-permute-start | bytes 221192 | tf_op jit(solution)/shard_map/ppermute | solution.py:387
  37.6 7.6 %collective-permute-start.6 = (bf16[4,8192]{1,0:T(4,128)(2,1)S(1)}, bf16[4,8192]{1,0:T(4,128)(2,1)S(1)}, u32[]{:S(2)}, u32[]{:S(2)}) collective-permute-start(bf16[4,8192]{1,0:T(4,128)(2,1)S(1)} %finish.1), channel_id=1, source_target_pairs={{0,8},{1,9},{2,10},{3,11},{4,12},{5,13},{6,14},{7,15},{8,0},{9,1},... | collective-permute-start | bytes 196616 | tf_op jit(solution)/shard_map/ppermute | solution.py:387
  39.6 5.6 %collective-permute-start.7 = (bf16[4,8192]{1,0:T(4,128)(2,1)S(1)}, bf16[4,8192]{1,0:T(4,128)(2,1)S(1)}, u32[]{:S(2)}, u32[]{:S(2)}) collective-permute-start(bf16[4,8192]{1,0:T(4,128)(2,1)S(1)} %finish.1), channel_id=1, source_target_pairs={{0,4},{1,5},{2,6},{3,7},{4,0},{5,1},{6,2},{7,3},{8,12},{9,13},{10,... | collective-permute-start | bytes 196616 | tf_op jit(solution)/shard_map/ppermute | solution.py:387
  40.0 6.2 %collective-permute-start.8 = (bf16[4,8192]{1,0:T(4,128)(2,1)S(1)}, bf16[4,8192]{1,0:T(4,128)(2,1)S(1)}, u32[]{:S(2)}, u32[]{:S(2)}) collective-permute-start(bf16[4,8192]{1,0:T(4,128)(2,1)S(1)} %finish.1), channel_id=1, source_target_pairs={{0,12},{1,13},{2,14},{3,15},{4,8},{5,9},{6,10},{7,11},{8,4},{9,5},... | collective-permute-start | bytes 196616 | tf_op jit(solution)/shard_map/ppermute | solution.py:387
  46.4 1.6 %collective-permute-start.9 = (bf16[16,8192]{1,0:T(8,128)(2,1)S(1)}, bf16[16,8192]{1,0:T(8,128)(2,1)S(1)}, u32[]{:S(2)}, u32[]{:S(2)}) collective-permute-start(bf16[16,8192]{1,0:T(8,128)(2,1)S(1)} %pad_maximum_fusion.near_ref), channel_id=1, source_target_pairs={{0,1},{1,0},{2,3},{3,2},{4,5},{5,4},{6,7},{7,6},{8,9},{9,8},{10,11... | collective-permute-start | bytes 786440 | tf_op jit(solution)/shard_map/ppermute | solution.py:417
  59.8 1.6 %collective-permute-start.10 = (bf16[16,8192]{1,0:T(8,128)(2,1)S(1)}, bf16[16,8192]{1,0:T(8,128)(2,1)S(1)}, u32[]{:S(2)}, u32[]{:S(2)}) collective-permute-start(bf16[16,8192]{1,0:T(8,128)(2,1)S(1)} %get-tuple-element.76), channel_id=1, source_target_pairs={{0,1},{1,0},{2,3},{3,2},{4,5},{5,4},{6,7},{7,6},{8,9},{9,8},{10,11... | collective-permute-start | bytes 786440 | tf_op jit(solution)/shard_map/ppermute | solution.py:417
  61.5 7.7 %collective-permute-start.11 = (bf16[4,8192]{1,0:T(4,128)(2,1)S(1)}, bf16[4,8192]{1,0:T(4,128)(2,1)S(1)}, u32[]{:S(2)}, u32[]{:S(2)}) collective-permute-start(bf16[4,8192]{1,0:T(4,128)(2,1)S(1)} %get-tuple-element.78), channel_id=1, source_target_pairs={{0,8},{1,9},{2,10},{3,11},{4,12},{5,13},{6,14},{7,15},{8,0},{9,1},... | collective-permute-start | bytes 196616 | tf_op jit(solution)/shard_map/ppermute | solution.py:387
  62.8 6.3 %collective-permute-start.12 = (bf16[4,8192]{1,0:T(4,128)(2,1)S(1)}, bf16[4,8192]{1,0:T(4,128)(2,1)S(1)}, u32[]{:S(2)}, u32[]{:S(2)}) collective-permute-start(bf16[4,8192]{1,0:T(4,128)(2,1)S(1)} %get-tuple-element.79), channel_id=1, source_target_pairs={{0,4},{1,5},{2,6},{3,7},{4,0},{5,1},{6,2},{7,3},{8,12},{9,13},{10,... | collective-permute-start | bytes 196616 | tf_op jit(solution)/shard_map/ppermute | solution.py:387
  64.1 6.1 %collective-permute-start.13 = (bf16[4,8192]{1,0:T(4,128)(2,1)S(1)}, bf16[4,8192]{1,0:T(4,128)(2,1)S(1)}, u32[]{:S(2)}, u32[]{:S(2)}) collective-permute-start(bf16[4,8192]{1,0:T(4,128)(2,1)S(1)} %get-tuple-element.80), channel_id=1, source_target_pairs={{0,12},{1,13},{2,14},{3,15},{4,8},{5,9},{6,10},{7,11},{8,4},{9,5},... | collective-permute-start | bytes 196616 | tf_op jit(solution)/shard_map/ppermute | solution.py:387
  70.3 4.0 %collective-permute-start.14 = (bf16[2,8192]{1,0:T(2,128)(2,1)S(1)}, bf16[2,8192]{1,0:T(2,128)(2,1)S(1)}, u32[]{:S(2)}, u32[]{:S(2)}) collective-permute-start(bf16[2,8192]{1,0:T(2,128)(2,1)S(1)} %get-tuple-element.82), channel_id=1, source_target_pairs={{0,2},{1,3},{2,0},{3,1},{4,6},{5,7},{6,4},{7,5},{8,10},{9,11},{10,... | collective-permute-start | bytes 98312 | tf_op jit(solution)/shard_map/ppermute | solution.py:387
